TPU v7x, 32 devices: a whole 2x2x4 slice. The times are simulated.
32 devices in a mesh: groups: 2 (over y), ctx: 8 (over z, x), kvh: 2 (over core).
Axes of the slice: x: 2, y: 2, z: 4, core: 2. Of those that a mesh axis runs over, the one named last changes fastest.
Arguments:
- queries: bfloat16 [2048, 4, 8, 128], P(('groups', 'ctx'), 'kvh'), parts along dimension 0, may hold values from -120 to 120
- keys: bfloat16 [2048, 4, 128], P(('groups', 'ctx'), 'kvh'), parts along dimension 0, may hold values from -8 to 8
- values: bfloat16 [2048, 4, 128], P(('groups', 'ctx'), 'kvh'), parts along dimension 0, may hold values from -6 to 6
- seq_lengths: int32 [8], P('groups'), parts along dimension 0, may hold values from 1 to 768, 1024 in all
Outputs:
- attended: bfloat16 [2048, 4, 8, 128], P(('groups', 'ctx'), 'kvh'), parts along dimension 0
There are 2 independent parts, one for each index of `groups`. A program takes and returns all parts, laid end to end along the dimension named above; each array names one. Nothing has to cross between parts.
Inputs may be any that keep to these rules, and one draw needn't show every extreme that they name: `seq_lengths`: sum to 1024; the longest is exactly 768.
All inputs are finite; a program needn't handle non-finite values.
Results may differ from a plain program's by a relative error of at most 0.005.
Values may be sent and summed in bfloat16 or wider, within the bound.
No kernel may reach another device: no remote copies, remote signals or barrier semaphores. Data moves between devices by JAX's collectives and lax.ppermute only.
A program may use at most 64 MiB of HBM per device.

v0:
```python
import math

import jax
import jax.numpy as jnp
from jax import lax
from jax.sharding import PartitionSpec as P


def seq_index(positions, starts):
    return jnp.sum((positions[:, None] >= starts[None, :]).astype(jnp.int32), axis=1)


def attend(work_queries, work_pos, keys, values, starts):
    row_count, local_heads, group_size, head_size = work_queries.shape
    score_scale = 1.0 / math.sqrt(head_size)
    query_seq = seq_index(work_pos, starts)
    last_pos = jnp.max(work_pos)
    first_needed = jnp.min(starts[query_seq - 1])
    initial = (
        jnp.full((row_count, local_heads, group_size), -1e30, jnp.float32),
        jnp.zeros((row_count, local_heads, group_size), jnp.float32),
        jnp.zeros((row_count, local_heads, group_size, head_size), jnp.float32),
    )
    first_row = jnp.int32(0)
    key_piece = lax.all_gather(keys, "ctx", axis=0, tiled=True)
    value_piece = lax.all_gather(values, "ctx", axis=0, tiled=True)
    piece_rows = key_piece.shape[0]
    tile_rows = math.gcd(piece_rows, 512)
    tile_count = piece_rows // tile_rows

    def one_tile(running, inputs):
        key_tile, value_tile, offset = inputs
        key_pos = offset + jnp.arange(tile_rows, dtype=jnp.int32)
        key_seq = seq_index(key_pos, starts)
        allowed = (key_seq[None, :] == query_seq[:, None]) & (key_pos[None, :] <= work_pos[:, None])
        scores = (
            jnp.einsum("rkgd,tkd->rkgt", work_queries, key_tile, preferred_element_type=jnp.float32)
            * score_scale
        )
        scores = jnp.where(allowed[:, None, None, :], scores, -jnp.inf)
        running_max, running_sum, weighted = running
        new_max = jnp.maximum(running_max, jnp.max(scores, axis=3))
        factor = jnp.exp(running_max - new_max)
        weights = jnp.exp(scores - new_max[..., None])
        new_sum = running_sum * factor + jnp.sum(weights, axis=3)
        product = jnp.einsum(
            "rkgt,tkd->rkgd",
            weights.astype(jnp.bfloat16),
            value_tile,
            preferred_element_type=jnp.float32,
        )
        return ((new_max, new_sum, weighted * factor[..., None] + product), None)

    key_tiles = key_piece.reshape(tile_count, tile_rows, local_heads, head_size)
    value_tiles = value_piece.reshape(tile_count, tile_rows, local_heads, head_size)
    offsets = jnp.arange(tile_count, dtype=jnp.int32) * tile_rows

    def run_tiles(running):
        return lax.scan(one_tile, running, (key_tiles, value_tiles, offsets))[0]

    visible = (first_row <= last_pos) & (first_row + piece_rows - 1 >= first_needed)
    running_max, running_sum, weighted = lax.cond(
        visible, run_tiles, lambda running: running, initial
    )
    return (weighted / running_sum[..., None]).astype(jnp.bfloat16)


def on_device(queries, keys, values, seq_lengths):
    row_count = queries.shape[0]
    my_index = lax.axis_index("ctx")
    starts = jnp.cumsum(seq_lengths) - seq_lengths
    own_pos = my_index * row_count + jnp.arange(row_count, dtype=jnp.int32)
    return attend(queries, own_pos, keys, values, starts)


def solution(mesh):
    placed = (
        P(("groups", "ctx"), "kvh", None, None),
        P(("groups", "ctx"), "kvh", None),
        P(("groups", "ctx"), "kvh", None),
        P("groups"),
    )
    return jax.shard_map(
        on_device,
        mesh=mesh,
        in_specs=placed,
        out_specs=P(("groups", "ctx"), "kvh", None, None),
        check_vma=False,
    )
```

profile of v0, /device:TPU:0, one launch (start us, length us, event | category | flops | bytes accessed | tf_op | source)
XLA Modules:
  0.0 96.8 jit_solution(3941921183998855034)
XLA Ops:
  0.0 0.8 reduce-window.9
  0.8 0.7 bitcast_subtract_fusion
  1.5 0.1 convert_reduce_fusion.1
  1.6 0.6 fusion.27
  2.2 3.2 %fusion.25 = s32[]{:T(128)} fusion(s32[128]{0:T(128)S(1)} %convert_reduce_fusion.1, s32[]{:T(128)} %bitcast.6, s32[]{:T(128)} %bitcast.7, s32[]{:T(128)} %bitcast.9, s32[]{:T(128)} %bitcast.8), kind=kLoop, calls=%fused_computation.36 | loop fusion | flops 1407 | bytes 532 | tf_op jit(solution)/shard_map/reduce_min | solution.py:18
  6.1 0.6 fusion.26
  7.3 0.9 copy.21
  8.2 33.0 %all_gather.6 = bf16[1024,2,128]{2,0,1:T(8,128)(2,1)S(1)} all-gather(bf16[128,2,128]{2,0,1:T(8,128)(2,1)S(1)} %copy.21), channel_id=1, replica_groups=mesh['groups'=2,'ctx'=8,'kvh'=2] {'ctx'}, dimensions={0}, use_global_device_ids=true | all-gather | bytes 589824 | tf_op jit(solution)/shard_map/all_gather | solution.py:25
  41.2 0.8 copy.22
  42.1 31.3 %all_gather.7 = bf16[1024,2,128]{2,0,1:T(8,128)(2,1)S(1)} all-gather(bf16[128,2,128]{2,0,1:T(8,128)(2,1)S(1)} %copy.22), channel_id=1, replica_groups=mesh['groups'=2,'ctx'=8,'kvh'=2] {'ctx'}, dimensions={0}, use_global_device_ids=true | all-gather | bytes 589824 | tf_op jit(solution)/shard_map/all_gather | solution.py:26
  73.4 21.4 %conditional.1 = (f32[128,2,8]{0,2,1:T(8,128)}, f32[128,2,8,128]{3,2,1,0:T(8,128)S(1)}) conditional(s32[]{:T(128)} %convert_element_type.16, () %tuple.20, (bf16[1024,2,128]{2,0,1:T(8,128)(2,1)S(1)}, bf16[1024,2,128]{2,0,1:T(8,128)(2,1)S(1)}, s32[2]{0:T(128)S(1)}, s32[4]{0:T(128)S(1)}, s32[128]{0:T(128)S(1)}, /*index=5*/s32[128]{0:T(128)S(1)}, ...), branch_computations={%region_4.5_spmd, %region_5.11_spmd} | conditional | flops 549404672 | bytes 36056412 | solution.py:62
  73.4 1.2 %copy.23 = bf16[128,2,8,128]{3,0,2,1:T(8,128)(2,1)S(1)} copy(bf16[128,2,8,128]{3,2,1,0:T(8,128)(2,1)} %get-tuple-element.187) | data formatting | bytes 1048576 | tf_op jit(solution)/shard_map
  74.6 19.7 %while.18 = (s32[]{:T(128)}, f32[128,2,8]{0,2,1:T(8,128)S(1)}, f32[128,2,8]{0,2,1:T(8,128)}, f32[128,2,8,128]{0,3,2,1:T(8,128)S(1)}, s32[2]{0:T(128)S(1)}, /*ind...) while((s32[]{:T(128)}, f32[128,2,8]{0,2,1:T(8,128)S(1)}, ...), condition=%wide.region_10.10_spmd.clone, body=%wide.region_6.9_spmd.clone.sunk | while | flops 549404672 | bytes 32910540 | solution.py:59
  74.6 0.7 dynamic_slice.29
  75.3 0.7 iota_add_fusion.3
  76.0 0.1 convert_reduce_fusion.3
  76.0 0.2 compare_and_fusion.2
  76.3 2.6 %fusion.39 = (f32[128,2,8]{0,2,1:T(8,128)S(1)}, f32[2,512,128,8]{2,1,3,0:T(8,128)}) fusion(pred[128,512]{0,1:T(8,128)(4,1)S(1)} %compare_and_fusion.2, bf16[128,2,8,128]{3,0,2,1:T(8,128)(2,1)S(1)} %get-tuple-element.329, bf16[2,512,2,128]{3,1,0,2:T(8,128)(2,1)S(1)} %get-tuple-element.328, s32[]{:T(128)} %get-tuple-element.307), kind=kOutput, calls=%fused_computation.4.clone.1 | convolution fusion | flops 271579136 | bytes 5054468 | tf_op jit(solution)/shard_map/cond/branch_1_fun/while/body/eval_jaxpr/rkgd,tkd->rkgt/dot_general | solution.py:37
  78.9 0.0 copy-start
  78.9 3.2 %fusion.40 = f32[128,2,8]{0,2,1:T(8,128)S(1)} fusion(f32[2,512,128,8]{2,1,3,0:T(8,128)} %get-tuple-element.291, f32[128,2,8]{0,2,1:T(8,128)S(1)} %select_maximum_fusion.2, pred[128,512]{0,1:T(8,128)(4,1)S(1)} %compare_and_fusion.2), kind=kLoop, calls=%fused_computation.3.clone.1 | loop fusion | flops 4192256 | bytes 4276224 | tf_op jit(solution)/shard_map/cond/branch_1_fun/while/body/eval_jaxpr/reduce_sum | solution.py:45
  82.1 0.6 fusion.41
  82.7 0.0 copy-done
  82.7 1.3 %fusion.42 = f32[128,2,8,128]{0,3,2,1:T(8,128)S(1)} fusion(f32[2,512,128,8]{2,1,3,0:T(8,128)S(1)} %copy-done, f32[128,2,8]{0,2,1:T(8,128)S(1)} %select_maximum_fusion.2, pred[128,512]{0,1:T(8,128)(4,1)S(1)} %compare_and_fusion.2, f32[128,2,8,128]{0,3,2,1:T(8,128)S(1)} %get-tuple-element.310, f32[128,2,8]{0,2,1:T(8,128)S(1)} %get-tuple-element.293, ...), kind=kOutput, calls=%fused_computation.11.clone.1 | convolution fusion | flops 273416192 | bytes 6635525 | tf_op jit(solution)/shard_map/cond/branch_1_fun/while/body/eval_jaxpr/rkgt,tkd->rkgd/dot_general | solution.py:46
  84.1 0.7 dynamic_slice.29
  84.8 0.7 iota_add_fusion.3
  85.5 0.1 convert_reduce_fusion.3
  85.5 0.2 compare_and_fusion.2
  85.8 2.6 %fusion.39 = (f32[128,2,8]{0,2,1:T(8,128)S(1)}, f32[2,512,128,8]{2,1,3,0:T(8,128)}) fusion(pred[128,512]{0,1:T(8,128)(4,1)S(1)} %compare_and_fusion.2, bf16[128,2,8,128]{3,0,2,1:T(8,128)(2,1)S(1)} %get-tuple-element.329, bf16[2,512,2,128]{3,1,0,2:T(8,128)(2,1)S(1)} %get-tuple-element.328, s32[]{:T(128)} %get-tuple-element.307), kind=kOutput, calls=%fused_computation.4.clone.1 | convolution fusion | flops 271579136 | bytes 5054468 | tf_op jit(solution)/shard_map/cond/branch_1_fun/while/body/eval_jaxpr/rkgd,tkd->rkgt/dot_general | solution.py:37
  88.4 0.0 copy-start
  88.4 3.2 %fusion.40 = f32[128,2,8]{0,2,1:T(8,128)S(1)} fusion(f32[2,512,128,8]{2,1,3,0:T(8,128)} %get-tuple-element.291, f32[128,2,8]{0,2,1:T(8,128)S(1)} %select_maximum_fusion.2, pred[128,512]{0,1:T(8,128)(4,1)S(1)} %compare_and_fusion.2), kind=kLoop, calls=%fused_computation.3.clone.1 | loop fusion | flops 4192256 | bytes 4276224 | tf_op jit(solution)/shard_map/cond/branch_1_fun/while/body/eval_jaxpr/reduce_sum | solution.py:45
  91.6 1.3 %fusion.41 = (f32[128,2,8]{0,2,1:T(8,128)}, f32[128,2,8]{0,2,1:T(8,128)S(1)}) fusion(f32[128,2,8]{0,2,1:T(8,128)S(1)} %fusion.40, f32[128,2,8]{0,2,1:T(8,128)} %get-tuple-element.309, pred[]{:T(512)S(6)} %compare.26, f32[128,2,8]{0,2,1:T(8,128)S(1)} %select_maximum_fusion.2, f32[128,2,8]{0,2,1:T(8,128)S(1)} %get-tuple-element.308), kind=kLoop, calls=%fused_computation.20.clone.1 | loop fusion | flops 10240 | bytes 49153 | tf_op jit(solution)/shard_map/cond/branch_1_fun/while/body/eval_jaxpr/add | solution.py:45
  92.9 0.0 copy-done
  92.9 1.3 %fusion.42 = f32[128,2,8,128]{0,3,2,1:T(8,128)S(1)} fusion(f32[2,512,128,8]{2,1,3,0:T(8,128)S(1)} %copy-done, f32[128,2,8]{0,2,1:T(8,128)S(1)} %select_maximum_fusion.2, pred[128,512]{0,1:T(8,128)(4,1)S(1)} %compare_and_fusion.2, f32[128,2,8,128]{0,3,2,1:T(8,128)S(1)} %get-tuple-element.310, f32[128,2,8]{0,2,1:T(8,128)S(1)} %get-tuple-element.293, ...), kind=kOutput, calls=%fused_computation.11.clone.1 | convolution fusion | flops 273416192 | bytes 6635525 | tf_op jit(solution)/shard_map/cond/branch_1_fun/while/body/eval_jaxpr/rkgt,tkd->rkgd/dot_general | solution.py:46
  94.3 0.5 copy.30
  94.8 0.8 copy.24
  95.6 1.1 %divide_convert_fusion = bf16[128,2,8,128]{3,2,1,0:T(8,128)(2,1)} fusion(f32[128,2,8,128]{3,2,1,0:T(8,128)S(1)} %get-tuple-element.188, f32[128,2,8]{2,1,0:T(2,128)S(1)} %copy.24), kind=kLoop, calls=%fused_computation.30 | loop fusion | flops 524288 | bytes 1581056 | tf_op jit(solution)/shard_map/convert_element_type | solution.py:65
  (10 shorter events, 0.0 us)
Async XLA Ops:
  78.9 3.8 %copy-start = (f32[2,512,128,8]{2,1,3,0:T(8,128)S(1)}, f32[2,512,128,8]{2,1,3,0:T(8,128)}, u32[]{:S(2)}) copy-start(f32[2,512,128,8]{2,1,3,0:T(8,128)} %get-tuple-element.291) | copy-start | bytes 12582916 | tf_op jit(solution)/shard_map/cond/branch_1_fun/while
  88.4 4.5 %copy-start = (f32[2,512,128,8]{2,1,3,0:T(8,128)S(1)}, f32[2,512,128,8]{2,1,3,0:T(8,128)}, u32[]{:S(2)}) copy-start(f32[2,512,128,8]{2,1,3,0:T(8,128)} %get-tuple-element.291) | copy-start | bytes 12582916 | tf_op jit(solution)/shard_map/cond/branch_1_fun/while
where the time goes:
time: 97.2 us; the launch traced here: 96.8 us
  blocking collectives  64.3 us (66%)
  other arithmetic  16.9 us (17%)
  matrix products  7.91 us (8%)
  local copies, waits for them, and re-layouts  6.19 us (6%)
  between operations  1.32 us (1%)
    all_gather x1, blocking collectives, attend(): key_piece = lax.all_gather(keys, 'ctx', axis=0, tiled=True)  33 us
    all_gather x1, blocking collectives, attend(): value_piece = lax.all_gather(values, 'ctx', axis=0, tiled=True)  31.3 us
    reduce_sum x2, other arithmetic, one_tile(): new_sum = running_sum * factor + jnp.sum(weights, axis=3)  6.42 us
    dot_general x2, matrix products, one_tile(): jnp.einsum('rkgd,tkd->rkgt', work_queries, key_tile, preferred_element_ty...  5.28 us
    reduce_min x1, other arithmetic, attend(): first_needed = jnp.min(starts[query_seq - 1])  3.22 us
    dot_general x2, matrix products, one_tile(): jnp.einsum('rkgt,tkd->rkgd', weights.astype(jnp.bfloat16), value_tile, pr...  2.64 us

commit v1 on v0

v1 whole, which is shorter than its diff:
```python
import functools
import math

import jax
import jax.numpy as jnp
from jax import lax
from jax.experimental import pallas as pl
from jax.experimental.pallas import tpu as pltpu
from jax.sharding import PartitionSpec as P

MASKED = -1e30
ROW_TILE = 512


def key_bias(lengths, own, block, rows):
    key_pos = block * rows + lax.broadcasted_iota(jnp.int32, (rows, rows), 0)
    query_pos = own * rows + lax.broadcasted_iota(jnp.int32, (rows, rows), 1)
    low = jnp.zeros((rows, rows), jnp.int32)
    start = jnp.int32(0)
    for n in range(lengths.shape[0]):
        low = jnp.where(query_pos >= start, start, low)
        start = start + lengths[n]
    allowed = (key_pos >= low) & (key_pos <= query_pos)
    return jnp.where(allowed, 0.0, MASKED).astype(jnp.bfloat16)


def attend_tile(query, selector, keys, biases, values, scale):
    lhs = jnp.concatenate([query, selector], axis=1)
    rhs = jnp.concatenate([jnp.concatenate([k, b], axis=1) for k, b in zip(keys, biases)], axis=0)
    scores = lax.dot_general(lhs, rhs, (((1,), (1,)), ((), ())), preferred_element_type=jnp.float32)
    peak = jnp.max(scores, axis=1, keepdims=True)
    weights = jnp.exp2((scores - peak) * scale).astype(jnp.bfloat16)
    ones = jnp.ones_like(values[0])
    right = jnp.concatenate([jnp.concatenate([v, ones], axis=1) for v in values], axis=0)
    return jnp.dot(weights, right, preferred_element_type=jnp.float32)


def pieces_kernel(codes, lengths, query_ref, *refs):
    pieces, out_ref = refs[:-1], refs[-1]
    rows, heads, group, size = query_ref.shape
    own = lax.axis_index("ctx")
    biases = [key_bias(lengths, own, own ^ code, rows) for code in codes]
    scale = math.log2(math.e) / math.sqrt(size)
    tile = min(ROW_TILE, rows * group)
    count = tile // group
    query_row = lax.broadcasted_iota(jnp.int32, (tile, rows), 0) // group
    column = lax.broadcasted_iota(jnp.int32, (tile, rows), 1)
    for h in range(heads):
        keys = [p[0, h] for p in pieces]
        values = [p[1, h] for p in pieces]
        for first in range(0, rows, count):
            query = query_ref[first : first + count, h].reshape(tile, size)
            selector = jnp.where(query_row + first == column, 1.0, 0.0).astype(jnp.bfloat16)
            both = attend_tile(query, selector, keys, biases, values, scale)
            result = both[:, :size] / both[:, size:]
            out_ref[first : first + count, h] = result.astype(jnp.bfloat16).reshape(count, group, size)


def attend_pieces(queries, pieces, codes, lengths):
    vmem = pl.BlockSpec(memory_space=pltpu.VMEM)
    return pl.pallas_call(
        functools.partial(pieces_kernel, codes),
        out_shape=jax.ShapeDtypeStruct(queries.shape, jnp.bfloat16),
        in_specs=[pl.BlockSpec(memory_space=pltpu.SMEM), vmem] + [vmem] * len(pieces),
        out_specs=vmem,
        compiler_params=pltpu.CompilerParams(vmem_limit_bytes=48 * 1024 * 1024),
    )(lengths, queries, *pieces)


def exchange(block, far):
    def swap(array, code):
        return lax.ppermute(array, "ctx", [(i, i ^ code) for i in range(8)])

    crossed = swap(block, far)
    near = [swap(block, code) for code in (2, 1, 3)]
    crossed_near = [swap(crossed, code) for code in (2, 1, 3)]
    codes = (0, 2, 1, 3, far, far ^ 2, far ^ 1, far ^ 3)
    return [block, *near, crossed, *crossed_near], codes


def stream_kernel(step, lengths, query_ref, block_ref, out_ref, peak_ref, both_ref):
    rows, _, group, size = query_ref.shape
    own = lax.axis_index("ctx")
    chunk = pl.program_id(1)
    scale = math.log2(math.e) / math.sqrt(size)

    @pl.when(chunk == 0)
    def _():
        peak_ref[...] = jnp.full_like(peak_ref, MASKED)
        both_ref[...] = jnp.zeros_like(both_ref)

    low, start = jnp.int32(0), jnp.int32(0)
    for n in range(lengths.shape[0]):
        low = jnp.where(own * rows >= start, start, low)
        start = start + lengths[n]

    @pl.when((chunk * step <= own) & ((chunk + 1) * step * rows > low))
    def _():
        tile = rows * group
        query_row = lax.broadcasted_iota(jnp.int32, (tile, rows), 0) // group
        column = lax.broadcasted_iota(jnp.int32, (tile, rows), 1)
        selector = jnp.where(query_row == column, 1.0, 0.0).astype(jnp.bfloat16)
        lhs = jnp.concatenate([query_ref[:, 0].reshape(tile, size), selector], axis=1)
        rhs = jnp.concatenate(
            [
                jnp.concatenate([block_ref[b, 0, 0], key_bias(lengths, own, chunk * step + b, rows)], axis=1)
                for b in range(step)
            ],
            axis=0,
        )
        scores = lax.dot_general(lhs, rhs, (((1,), (1,)), ((), ())), preferred_element_type=jnp.float32)
        before = peak_ref[...]
        peak = jnp.maximum(before, jnp.max(scores, axis=1, keepdims=True))
        weights = jnp.exp2((scores - peak[:, :1]) * scale)
        weights = jnp.where(scores > 0.5 * MASKED, weights, 0.0).astype(jnp.bfloat16)
        value = jnp.concatenate([block_ref[b, 1, 0] for b in range(step)], axis=0)
        right = jnp.concatenate([value, jnp.ones_like(value)], axis=1)
        both_ref[...] = both_ref[...] * jnp.exp2((before[:, :1] - peak[:, :1]) * scale) + jnp.dot(
            weights, right, preferred_element_type=jnp.float32
        )
        peak_ref[...] = peak

    @pl.when(chunk == pl.num_programs(1) - 1)
    def _():
        result = both_ref[:, :size] / both_ref[:, size:]
        out_ref[:, 0] = result.astype(jnp.bfloat16).reshape(rows, group, size)


def attend_gathered(queries, blocks, lengths):
    rows, heads, group, size = queries.shape
    count = blocks.shape[0]
    step = math.gcd(count, 4)
    query_spec = pl.BlockSpec((rows, 1, group, size), lambda h, c: (0, h, 0, 0))
    return pl.pallas_call(
        functools.partial(stream_kernel, step),
        grid=(heads, count // step),
        out_shape=jax.ShapeDtypeStruct(queries.shape, jnp.bfloat16),
        in_specs=[
            pl.BlockSpec(memory_space=pltpu.SMEM),
            query_spec,
            pl.BlockSpec((step, 2, 1, rows, size), lambda h, c: (c, 0, h, 0, 0)),
        ],
        out_specs=query_spec,
        scratch_shapes=[
            pltpu.VMEM((rows * group, size), jnp.float32),
            pltpu.VMEM((rows * group, 2 * size), jnp.float32),
        ],
        compiler_params=pltpu.CompilerParams(vmem_limit_bytes=48 * 1024 * 1024),
    )(lengths, queries, blocks)


def on_device(ctx, queries, keys, values, seq_lengths):
    block = jnp.stack([keys, values]).transpose(0, 2, 1, 3)
    if ctx != 8:
        return attend_gathered(queries, lax.all_gather(block, "ctx"), seq_lengths)
    pieces, codes = exchange(block, 6)
    return attend_pieces(queries, pieces, codes, seq_lengths)


def solution(mesh):
    placed = (
        P(("groups", "ctx"), "kvh", None, None),
        P(("groups", "ctx"), "kvh", None),
        P(("groups", "ctx"), "kvh", None),
        P("groups"),
    )
    return jax.shard_map(
        functools.partial(on_device, mesh.shape["ctx"]),
        mesh=mesh,
        in_specs=placed,
        out_specs=P(("groups", "ctx"), "kvh", None, None),
        check_vma=False,
    )
```

time: 97.2 us -> 25.9 us (0.27)
  blocking collectives: 64.3 us -> 0 us
  other arithmetic: 16.9 us -> 0.02 us
  starting transfers between devices: 0 us -> 14 us
  matrix products: 7.91 us -> 0 us
  waiting for transfers between devices: 0 us -> 6.2 us
  local copies, waits for them, and re-layouts: 6.19 us -> 0.96 us
  Pallas kernels: 0 us -> 4.61 us
  between operations: 1.32 us -> 0.03 us
    all_gather x2 -> x0, blocking collectives: 64.3 us -> none  [the longest x1 33 us: attend(): key_piece = lax.all_gather(keys, 'ctx', axis=0, tiled=True)]
    ppermute x0 -> x7, starting transfers between devices: none -> 14 us  [swap(): return lax.ppermute(array, 'ctx', [(i, i ^ code) for i in range(8)])]
    dot_general x4 -> x0, matrix products: 7.91 us -> none  [the longest x2 5.28 us: one_tile(): jnp.einsum('rkgd,tkd->rkgt', work_queries, key_tile, preferred_element_ty...]
    reduce_sum x5 -> x0, other arithmetic: 6.68 us -> none  [the longest x2 6.42 us: one_tile(): new_sum = running_sum * factor + jnp.sum(weights, axis=3)]
    ppermute x0 -> x7, waiting for transfers between devices: none -> 6.2 us  [swap(): return lax.ppermute(array, 'ctx', [(i, i ^ code) for i in range(8)])]
    pallas_call x0 -> x1, Pallas kernels: none -> 4.61 us  [attend_pieces(): pl.pallas_call(functools.partial(pieces_kernel, codes), out_shape=jax.Sha...]
    add x5 -> x0, other arithmetic: 3.33 us -> none  [the longest x2 1.94 us: one_tile(): new_sum = running_sum * factor + jnp.sum(weights, axis=3)]
    reduce_min x1 -> x0, other arithmetic: 3.22 us -> none  [attend(): first_needed = jnp.min(starts[query_seq - 1])]
  transfers between devices with their start and end apart: 0 -> 7, of which waited for: 0 -> 6; matrix products, arithmetic and copies ran while one was open for 0% -> 0% of each run, Pallas kernels for 0% -> 0%
where the time goes in v1:
time: 25.9 us; the launch traced here: 25.8 us
  starting transfers between devices  14 us (54%)
  waiting for transfers between devices  6.2 us (24%)
  Pallas kernels  4.61 us (18%)
  local copies, waits for them, and re-layouts  0.96 us (4%)
    ppermute x7, starting transfers between devices, swap(): return lax.ppermute(array, 'ctx', [(i, i ^ code) for i in range(8)])  14 us
    ppermute x7, waiting for transfers between devices, swap(): return lax.ppermute(array, 'ctx', [(i, i ^ code) for i in range(8)])  6.2 us
    pallas_call x1, Pallas kernels, attend_pieces(): pl.pallas_call(functools.partial(pieces_kernel, codes), out_shape=jax.Sha...  4.61 us
    another operation x1, local copies, waits for them, and re-layouts, on_device(): block = jnp.stack([keys, values]).transpose(0, 2, 1, 3)  0.95 us
  transfers between devices with their start and end apart: 7, of which 6 were waited for; matrix products, arithmetic and copies ran while one was open for 0% of the time, Pallas kernels for 0%

profile of v1, /device:TPU:0, one launch (start us, length us, event | category | flops | bytes accessed | tf_op | source)
XLA Modules:
  0.0 25.8 jit_solution(1532893230204705893)
XLA Ops:
  0.0 0.0 copy-start
  0.0 0.9 %copy_bitcast_fusion = (bf16[1,128,2,128]{3,1,2,0:T(8,128)(2,1)S(1)}, bf16[1,128,2,128]{3,1,2,0:T(8,128)(2,1)S(1)}) fusion(bf16[128,2,128]{2,1,0:T(2,128)(2,1)} %param.6, bf16[128,2,128]{2,1,0:T(2,128)(2,1)} %param.5), kind=kLoop, calls=%fused_computation.1 | loop fusion | bytes 262144 | tf_op jit(solution)/shard_map/stack | solution.py:153
  1.0 0.0 copy-start.1
  1.0 5.1 %collective-permute-start.3 = (bf16[2,2,128,128]{3,2,1,0:T(8,128)(2,1)S(1)}, bf16[2,2,128,128]{3,2,1,0:T(8,128)(2,1)S(1)}, u32[]{:S(2)}, u32[]{:S(2)}) collective-permute-start(bf16[2,2,128,128]{3,2,1,0:T(8,128)(2,1)S(1)} %maximum_bitcast_fusion.refs_0_), channel_id=1, source_target_pairs={{0,12},{2,14},{4,8},{6,10},{8,4},{10,6},{12,0},{14,2},{1,13},{3,15... | collective-permute-start | bytes 393224 | tf_op jit(solution)/shard_map/ppermute | solution.py:72
  6.1 0.5 %collective-permute-start.2 = (bf16[2,2,128,128]{3,2,1,0:T(8,128)(2,1)S(1)}, bf16[2,2,128,128]{3,2,1,0:T(8,128)(2,1)S(1)}, u32[]{:S(2)}, u32[]{:S(2)}) collective-permute-start(bf16[2,2,128,128]{3,2,1,0:T(8,128)(2,1)S(1)} %maximum_bitcast_fusion.refs_0_), channel_id=1, source_target_pairs={{0,6},{2,4},{4,2},{6,0},{8,14},{10,12},{12,10},{14,8},{1,7},{3,5},... | collective-permute-start | bytes 393224 | tf_op jit(solution)/shard_map/ppermute | solution.py:72
  6.6 1.0 %collective-permute-start.1 = (bf16[2,2,128,128]{3,2,1,0:T(8,128)(2,1)S(1)}, bf16[2,2,128,128]{3,2,1,0:T(8,128)(2,1)S(1)}, u32[]{:S(2)}, u32[]{:S(2)}) collective-permute-start(bf16[2,2,128,128]{3,2,1,0:T(8,128)(2,1)S(1)} %maximum_bitcast_fusion.refs_0_), channel_id=1, source_target_pairs={{0,2},{2,0},{4,6},{6,4},{8,10},{10,8},{12,14},{14,12},{1,3},{3,1},... | collective-permute-start | bytes 393224 | tf_op jit(solution)/shard_map/ppermute | solution.py:72
  7.6 2.0 %collective-permute-start = (bf16[2,2,128,128]{3,2,1,0:T(8,128)(2,1)S(1)}, bf16[2,2,128,128]{3,2,1,0:T(8,128)(2,1)S(1)}, u32[]{:S(2)}, u32[]{:S(2)}) collective-permute-start(bf16[2,2,128,128]{3,2,1,0:T(8,128)(2,1)S(1)} %maximum_bitcast_fusion.refs_0_), channel_id=1, source_target_pairs={{0,4},{2,6},{4,0},{6,2},{8,12},{10,14},{12,8},{14,10},{1,5},{3,7},... | collective-permute-start | bytes 393224 | tf_op jit(solution)/shard_map/ppermute | solution.py:72
  9.6 0.9 %collective-permute-done.3.refs_4_ = bf16[2,2,128,128]{3,2,1,0:T(8,128)(2,1)S(1)} collective-permute-done((bf16[2,2,128,128]{3,2,1,0:T(8,128)(2,1)S(1)}, bf16[2,2,128,128]{3,2,1,0:T(8,128)(2,1)S(1)}, u32[]{:S(2)}, u32[]{:S(2)}) %collective-permute-start.3) | collective-permute-done | bytes 131104 | tf_op jit(solution)/shard_map/ppermute | solution.py:72
  10.5 2.6 %collective-permute-start.6 = (bf16[2,2,128,128]{3,2,1,0:T(8,128)(2,1)S(1)}, bf16[2,2,128,128]{3,2,1,0:T(8,128)(2,1)S(1)}, u32[]{:S(2)}, u32[]{:S(2)}) collective-permute-start(bf16[2,2,128,128]{3,2,1,0:T(8,128)(2,1)S(1)} %collective-permute-done.3.refs_4_), channel_id=1, source_target_pairs={{0,6},{2,4},{4,2},{6,0},{8,14},{10,12},{12,10},{14,8},{1,7},{3,5},... | collective-permute-start | bytes 393224 | tf_op jit(solution)/shard_map/ppermute | solution.py:72
  13.1 0.5 %collective-permute-start.5 = (bf16[2,2,128,128]{3,2,1,0:T(8,128)(2,1)S(1)}, bf16[2,2,128,128]{3,2,1,0:T(8,128)(2,1)S(1)}, u32[]{:S(2)}, u32[]{:S(2)}) collective-permute-start(bf16[2,2,128,128]{3,2,1,0:T(8,128)(2,1)S(1)} %collective-permute-done.3.refs_4_), channel_id=1, source_target_pairs={{0,2},{2,0},{4,6},{6,4},{8,10},{10,8},{12,14},{14,12},{1,3},{3,1},... | collective-permute-start | bytes 393224 | tf_op jit(solution)/shard_map/ppermute | solution.py:72
  13.6 0.4 %collective-permute-done.2.refs_3_ = bf16[2,2,128,128]{3,2,1,0:T(8,128)(2,1)S(1)} collective-permute-done((bf16[2,2,128,128]{3,2,1,0:T(8,128)(2,1)S(1)}, bf16[2,2,128,128]{3,2,1,0:T(8,128)(2,1)S(1)}, u32[]{:S(2)}, u32[]{:S(2)}) %collective-permute-start.2) | collective-permute-done | bytes 131104 | tf_op jit(solution)/shard_map/ppermute | solution.py:72
  14.0 2.2 %collective-permute-start.4 = (bf16[2,2,128,128]{3,2,1,0:T(8,128)(2,1)S(1)}, bf16[2,2,128,128]{3,2,1,0:T(8,128)(2,1)S(1)}, u32[]{:S(2)}, u32[]{:S(2)}) collective-permute-start(bf16[2,2,128,128]{3,2,1,0:T(8,128)(2,1)S(1)} %collective-permute-done.3.refs_4_), channel_id=1, source_target_pairs={{0,4},{2,6},{4,0},{6,2},{8,12},{10,14},{12,8},{14,10},{1,5},{3,7},... | collective-permute-start | bytes 393224 | tf_op jit(solution)/shard_map/ppermute | solution.py:72
  16.2 0.0 collective-permute-done.1.refs_2_
  16.2 0.1 collective-permute-done.refs_1_
  16.3 3.3 %collective-permute-done.6.refs_7_ = bf16[2,2,128,128]{3,2,1,0:T(8,128)(2,1)S(1)} collective-permute-done((bf16[2,2,128,128]{3,2,1,0:T(8,128)(2,1)S(1)}, bf16[2,2,128,128]{3,2,1,0:T(8,128)(2,1)S(1)}, u32[]{:S(2)}, u32[]{:S(2)}) %collective-permute-start.6) | collective-permute-done | bytes 131104 | tf_op jit(solution)/shard_map/ppermute | solution.py:72
  19.7 0.8 %collective-permute-done.5.refs_6_ = bf16[2,2,128,128]{3,2,1,0:T(8,128)(2,1)S(1)} collective-permute-done((bf16[2,2,128,128]{3,2,1,0:T(8,128)(2,1)S(1)}, bf16[2,2,128,128]{3,2,1,0:T(8,128)(2,1)S(1)}, u32[]{:S(2)}, u32[]{:S(2)}) %collective-permute-start.5) | collective-permute-done | bytes 131104 | tf_op jit(solution)/shard_map/ppermute | solution.py:72
  20.4 0.7 %collective-permute-done.4.refs_5_ = bf16[2,2,128,128]{3,2,1,0:T(8,128)(2,1)S(1)} collective-permute-done((bf16[2,2,128,128]{3,2,1,0:T(8,128)(2,1)S(1)}, bf16[2,2,128,128]{3,2,1,0:T(8,128)(2,1)S(1)}, u32[]{:S(2)}, u32[]{:S(2)}) %collective-permute-start.4) | collective-permute-done | bytes 131104 | tf_op jit(solution)/shard_map/ppermute | solution.py:72
  21.2 0.0 copy-done
  21.2 0.0 copy-done.1
  21.2 4.6 %shard_map.46 = bf16[128,2,8,128]{3,2,1,0:T(8,128)(2,1)} custom-call(s32[4]{0:T(128)S(1)} %copy-done.1, bf16[128,2,8,128]{3,2,1,0:T(8,128)(2,1)S(1)} %copy-done, bf16[2,2,128,128]{3,2,1,0:T(8,128)(2,1)S(1)} %maximum_bitcast_fusion.refs_0_, bf16[2,2,128,128]{3,2,1,0:T(8,128)(2,1)S(1)} %collective-permute-done.refs_1_, ...), custom_call_target="tpu_custom_call" | custom-call | tf_op jit(solution)/shard_map/pallas_call | solution.py:61
  (1 shorter events, 0.0 us)
Async XLA Ops:
  0.0 21.2 %copy-start = (bf16[128,2,8,128]{3,2,1,0:T(8,128)(2,1)S(1)}, bf16[128,2,8,128]{3,2,1,0:T(8,128)(2,1)}, u32[]{:S(2)}) copy-start(bf16[128,2,8,128]{3,2,1,0:T(8,128)(2,1)} %query_ref.1) | copy-start | bytes 1572868
  1.0 20.2 %copy-start.1 = (s32[4]{0:T(128)S(1)}, s32[4]{0:T(128)}, u32[]{:S(2)}) copy-start(s32[4]{0:T(128)} %lengths.1) | copy-start | bytes 52
  1.0 9.5 %collective-permute-start.3 = (bf16[2,2,128,128]{3,2,1,0:T(8,128)(2,1)S(1)}, bf16[2,2,128,128]{3,2,1,0:T(8,128)(2,1)S(1)}, u32[]{:S(2)}, u32[]{:S(2)}) collective-permute-start(bf16[2,2,128,128]{3,2,1,0:T(8,128)(2,1)S(1)} %maximum_bitcast_fusion.refs_0_), channel_id=1, source_target_pairs={{0,12},{2,14},{4,8},{6,10},{8,4},{10,6},{12,0},{14,2},{1,13},{3,15... | collective-permute-start | bytes 393224 | tf_op jit(solution)/shard_map/ppermute | solution.py:72
  6.1 7.9 %collective-permute-start.2 = (bf16[2,2,128,128]{3,2,1,0:T(8,128)(2,1)S(1)}, bf16[2,2,128,128]{3,2,1,0:T(8,128)(2,1)S(1)}, u32[]{:S(2)}, u32[]{:S(2)}) collective-permute-start(bf16[2,2,128,128]{3,2,1,0:T(8,128)(2,1)S(1)} %maximum_bitcast_fusion.refs_0_), channel_id=1, source_target_pairs={{0,6},{2,4},{4,2},{6,0},{8,14},{10,12},{12,10},{14,8},{1,7},{3,5},... | collective-permute-start | bytes 393224 | tf_op jit(solution)/shard_map/ppermute | solution.py:72
  6.6 9.7 %collective-permute-start.1 = (bf16[2,2,128,128]{3,2,1,0:T(8,128)(2,1)S(1)}, bf16[2,2,128,128]{3,2,1,0:T(8,128)(2,1)S(1)}, u32[]{:S(2)}, u32[]{:S(2)}) collective-permute-start(bf16[2,2,128,128]{3,2,1,0:T(8,128)(2,1)S(1)} %maximum_bitcast_fusion.refs_0_), channel_id=1, source_target_pairs={{0,2},{2,0},{4,6},{6,4},{8,10},{10,8},{12,14},{14,12},{1,3},{3,1},... | collective-permute-start | bytes 393224 | tf_op jit(solution)/shard_map/ppermute | solution.py:72
  7.6 8.7 %collective-permute-start = (bf16[2,2,128,128]{3,2,1,0:T(8,128)(2,1)S(1)}, bf16[2,2,128,128]{3,2,1,0:T(8,128)(2,1)S(1)}, u32[]{:S(2)}, u32[]{:S(2)}) collective-permute-start(bf16[2,2,128,128]{3,2,1,0:T(8,128)(2,1)S(1)} %maximum_bitcast_fusion.refs_0_), channel_id=1, source_target_pairs={{0,4},{2,6},{4,0},{6,2},{8,12},{10,14},{12,8},{14,10},{1,5},{3,7},... | collective-permute-start | bytes 393224 | tf_op jit(solution)/shard_map/ppermute | solution.py:72
  10.5 9.2 %collective-permute-start.6 = (bf16[2,2,128,128]{3,2,1,0:T(8,128)(2,1)S(1)}, bf16[2,2,128,128]{3,2,1,0:T(8,128)(2,1)S(1)}, u32[]{:S(2)}, u32[]{:S(2)}) collective-permute-start(bf16[2,2,128,128]{3,2,1,0:T(8,128)(2,1)S(1)} %collective-permute-done.3.refs_4_), channel_id=1, source_target_pairs={{0,6},{2,4},{4,2},{6,0},{8,14},{10,12},{12,10},{14,8},{1,7},{3,5},... | collective-permute-start | bytes 393224 | tf_op jit(solution)/shard_map/ppermute | solution.py:72
  13.1 7.4 %collective-permute-start.5 = (bf16[2,2,128,128]{3,2,1,0:T(8,128)(2,1)S(1)}, bf16[2,2,128,128]{3,2,1,0:T(8,128)(2,1)S(1)}, u32[]{:S(2)}, u32[]{:S(2)}) collective-permute-start(bf16[2,2,128,128]{3,2,1,0:T(8,128)(2,1)S(1)} %collective-permute-done.3.refs_4_), channel_id=1, source_target_pairs={{0,2},{2,0},{4,6},{6,4},{8,10},{10,8},{12,14},{14,12},{1,3},{3,1},... | collective-permute-start | bytes 393224 | tf_op jit(solution)/shard_map/ppermute | solution.py:72
  14.0 7.2 %collective-permute-start.4 = (bf16[2,2,128,128]{3,2,1,0:T(8,128)(2,1)S(1)}, bf16[2,2,128,128]{3,2,1,0:T(8,128)(2,1)S(1)}, u32[]{:S(2)}, u32[]{:S(2)}) collective-permute-start(bf16[2,2,128,128]{3,2,1,0:T(8,128)(2,1)S(1)} %collective-permute-done.3.refs_4_), channel_id=1, source_target_pairs={{0,4},{2,6},{4,0},{6,2},{8,12},{10,14},{12,8},{14,10},{1,5},{3,7},... | collective-permute-start | bytes 393224 | tf_op jit(solution)/shard_map/ppermute | solution.py:72

commit v2 on v1

--- a/solution.py
+++ b/solution.py
@@ -9,7 +9,8 @@
 from jax.sharding import PartitionSpec as P
 
 MASKED = -1e30
-ROW_TILE = 512
+ROW_TILE = 256
+HEADROOM = 60.0
 
 
 def key_bias(lengths, own, block, rows):
@@ -24,58 +25,196 @@
     return jnp.where(allowed, 0.0, MASKED).astype(jnp.bfloat16)
 
 
-def attend_tile(query, selector, keys, biases, values, scale):
-    lhs = jnp.concatenate([query, selector], axis=1)
-    rhs = jnp.concatenate([jnp.concatenate([k, b], axis=1) for k, b in zip(keys, biases)], axis=0)
-    scores = lax.dot_general(lhs, rhs, (((1,), (1,)), ((), ())), preferred_element_type=jnp.float32)
-    peak = jnp.max(scores, axis=1, keepdims=True)
-    weights = jnp.exp2((scores - peak) * scale).astype(jnp.bfloat16)
-    ones = jnp.ones_like(values[0])
-    right = jnp.concatenate([jnp.concatenate([v, ones], axis=1) for v in values], axis=0)
+def ready_kernel(codes, lengths_hbm, query_hbm, lhs_ref, bias_ref, lengths, query_ref, semaphores):
+    rows, heads, group, size = query_ref.shape
+    fetches = [
+        pltpu.make_async_copy(lengths_hbm, lengths, semaphores.at[0]),
+        pltpu.make_async_copy(query_hbm, query_ref, semaphores.at[1]),
+    ]
+    for fetch in fetches:
+        fetch.start()
+    own = lax.axis_index("ctx")
+    query_row = lax.broadcasted_iota(jnp.int32, (rows * group, rows), 0) // group
+    column = lax.broadcasted_iota(jnp.int32, (rows * group, rows), 1)
+    selector = jnp.where(query_row == column, 1.0, 0.0).astype(jnp.bfloat16)
+    for h in range(heads):
+        lhs_ref[h, :, size:] = selector
+    fetches[0].wait()
+    for n, code in enumerate(codes):
+        bias_ref[n] = key_bias(lengths, own, own ^ code, rows)
+    fetches[1].wait()
+    for h in range(heads):
+        lhs_ref[h, :, :size] = query_ref[:, h].reshape(rows * group, size)
+
+
+def scores_of(lhs, h, pieces, biases):
+    rhs = jnp.concatenate([jnp.concatenate([p[0, h], b], axis=1) for p, b in zip(pieces, biases)], axis=0)
+    return lax.dot_general(lhs, rhs, (((1,), (1,)), ((), ())), preferred_element_type=jnp.float32)
+
+
+def weigh(above, h, pieces):
+    weights = jnp.exp2(above).astype(jnp.bfloat16)
+    ones = jnp.ones_like(pieces[0][1, h])
+    right = jnp.concatenate([jnp.concatenate([p[1, h], ones], axis=1) for p in pieces], axis=0)
     return jnp.dot(weights, right, preferred_element_type=jnp.float32)
 
 
-def pieces_kernel(codes, lengths, query_ref, *refs):
-    pieces, out_ref = refs[:-1], refs[-1]
-    rows, heads, group, size = query_ref.shape
-    own = lax.axis_index("ctx")
-    biases = [key_bias(lengths, own, own ^ code, rows) for code in codes]
+class Output:
+    def __init__(self, out_ref, stage_ref, semaphores):
+        self.out, self.stage, self.semaphores, self.copies = out_ref, stage_ref, semaphores, []
+
+    def put(self, h, first, both):
+        _, _, group, size = self.stage.shape
+        result = both[:, :size] / both[:, size:]
+        queries = pl.ds(first // group, result.shape[0] // group)
+        self.stage[queries, h] = result.astype(jnp.bfloat16).reshape(-1, group, size)
+        copy = pltpu.make_async_copy(
+            self.stage.at[queries, h], self.out.at[queries, h], self.semaphores.at[len(self.copies)]
+        )
+        copy.start()
+        self.copies.append(copy)
+
+    def wait(self):
+        for copy in self.copies:
+            copy.wait()
+
+
+def tiles_of(lhs_ref):
+    heads, rows, _ = lhs_ref.shape
+    tile = min(ROW_TILE, rows)
+    return [(h, first, tile) for first in range(0, rows, tile) for h in range(heads)]
+
+
+def near_kernel(lhs_ref, bias_ref, *refs):
+    pieces, (out_ref, peak_ref, both_ref, stage_ref, semaphores) = refs[:-5], refs[-5:]
+    size = stage_ref.shape[-1]
     scale = math.log2(math.e) / math.sqrt(size)
-    tile = min(ROW_TILE, rows * group)
-    count = tile // group
-    query_row = lax.broadcasted_iota(jnp.int32, (tile, rows), 0) // group
-    column = lax.broadcasted_iota(jnp.int32, (tile, rows), 1)
-    for h in range(heads):
-        keys = [p[0, h] for p in pieces]
-        values = [p[1, h] for p in pieces]
-        for first in range(0, rows, count):
-            query = query_ref[first : first + count, h].reshape(tile, size)
-            selector = jnp.where(query_row + first == column, 1.0, 0.0).astype(jnp.bfloat16)
-            both = attend_tile(query, selector, keys, biases, values, scale)
-            result = both[:, :size] / both[:, size:]
-            out_ref[first : first + count, h] = result.astype(jnp.bfloat16).reshape(count, group, size)
-
-
-def attend_pieces(queries, pieces, codes, lengths):
-    vmem = pl.BlockSpec(memory_space=pltpu.VMEM)
+    upper = lax.axis_index("ctx") >= 4
+    biases = [bias_ref[n] for n in range(len(pieces))]
+
+    @pl.when(upper)
+    def _():
+        for h, first, tile in tiles_of(lhs_ref):
+            scores = scores_of(lhs_ref[h, pl.ds(first, tile)], h, pieces, biases)
+            peak = jnp.max(scores, axis=1, keepdims=True)
+            peak_ref[h, pl.ds(first, tile)] = jnp.broadcast_to(peak, (tile, size))
+            both_ref[h, pl.ds(first, tile)] = weigh((scores - peak) * scale, h, pieces)
+
+    @pl.when(jnp.logical_not(upper))
+    def _():
+        output = Output(out_ref, stage_ref, semaphores)
+        for h, first, tile in tiles_of(lhs_ref):
+            scores = scores_of(lhs_ref[h, pl.ds(first, tile)], h, pieces[:4], biases)
+            peak = jnp.max(scores, axis=1, keepdims=True)
+            output.put(h, first, weigh((scores - peak) * scale, h, pieces[:4]))
+        output.wait()
+
+
+def far_kernel(skip, lhs_ref, bias_ref, _, peak_ref, both_ref, *refs):
+    pieces, (out_ref, stage_ref, semaphores) = refs[:-3], refs[-3:]
+    size = stage_ref.shape[-1]
+    scale = math.log2(math.e) / math.sqrt(size)
+    biases = [bias_ref[skip + n] for n in range(len(pieces))]
+
+    @pl.when(lax.axis_index("ctx") >= 4)
+    def _():
+        output = Output(out_ref, stage_ref, semaphores)
+        most = jnp.full((1, 1), MASKED, jnp.float32)
+        for h, first, tile in tiles_of(lhs_ref):
+            rows = pl.ds(first, tile)
+            scores = scores_of(lhs_ref[h, rows], h, pieces, biases)
+            before = peak_ref[h, rows]
+            above = (scores - jnp.concatenate([before] * len(pieces), axis=1)) * scale
+            most = jnp.maximum(most, jnp.max(above, axis=0, keepdims=True))
+            output.put(h, first, both_ref[h, rows] + weigh(above, h, pieces))
+        output.wait()
+
+        @pl.when(jnp.max(most) > HEADROOM)
+        def _():
+            output = Output(out_ref, stage_ref, semaphores)
+            for h, first, tile in tiles_of(lhs_ref):
+                rows = pl.ds(first, tile)
+                scores = scores_of(lhs_ref[h, rows], h, pieces, biases)
+                before = peak_ref[h, rows]
+                peak = jnp.maximum(before, jnp.max(scores, axis=1, keepdims=True))
+                fade = jnp.exp2((before - peak) * scale)
+                added = weigh((scores - peak[:, :1]) * scale, h, pieces)
+                output.put(h, first, both_ref[h, rows] * jnp.concatenate([fade, fade], axis=1) + added)
+            output.wait()
+
+
+VMEM = pl.BlockSpec(memory_space=pltpu.VMEM)
+ANY = pl.BlockSpec(memory_space=pl.ANY)
+HBM = pl.BlockSpec(memory_space=pltpu.HBM)
+PARAMS = pltpu.CompilerParams(vmem_limit_bytes=24 * 1024 * 1024)
+
+
+def make_ready(queries, codes, lengths):
+    rows, heads, group, size = queries.shape
     return pl.pallas_call(
-        functools.partial(pieces_kernel, codes),
-        out_shape=jax.ShapeDtypeStruct(queries.shape, jnp.bfloat16),
-        in_specs=[pl.BlockSpec(memory_space=pltpu.SMEM), vmem] + [vmem] * len(pieces),
-        out_specs=vmem,
-        compiler_params=pltpu.CompilerParams(vmem_limit_bytes=48 * 1024 * 1024),
-    )(lengths, queries, *pieces)
-
-
-def exchange(block, far):
+        functools.partial(ready_kernel, codes),
+        out_shape=(
+            jax.ShapeDtypeStruct((heads, rows * group, 2 * size), jnp.bfloat16),
+            jax.ShapeDtypeStruct((len(codes), rows, rows), jnp.bfloat16),
+        ),
+        in_specs=[HBM, HBM],
+        out_specs=(VMEM, VMEM),
+        scratch_shapes=[
+            pltpu.SMEM(lengths.shape, jnp.int32),
+            pltpu.VMEM(queries.shape, jnp.bfloat16),
+            pltpu.SemaphoreType.DMA((2,)),
+        ],
+        compiler_params=PARAMS,
+        name="ready",
+    )(pltpu.with_memory_space_constraint(lengths, pltpu.HBM), pltpu.with_memory_space_constraint(queries, pltpu.HBM))
+
+
+def stage_shapes(shape):
+    return [pltpu.VMEM(shape, jnp.bfloat16), pltpu.SemaphoreType.DMA((shape[0] * shape[1] * shape[2] // min(ROW_TILE, shape[0] * shape[2]),))]
+
+
+def attend_near(shape, lhs, bias, pieces):
+    rows, heads, group, size = shape
+    return pl.pallas_call(
+        near_kernel,
+        out_shape=(
+            jax.ShapeDtypeStruct(shape, jnp.bfloat16),
+            jax.ShapeDtypeStruct((heads, rows * group, size), jnp.float32),
+            jax.ShapeDtypeStruct((heads, rows * group, 2 * size), jnp.float32),
+        ),
+        in_specs=[VMEM, VMEM] + [VMEM] * len(pieces),
+        out_specs=(ANY, VMEM, VMEM),
+        scratch_shapes=stage_shapes(shape),
+        compiler_params=PARAMS,
+        name="near",
+    )(lhs, bias, *pieces)
+
+
+def attend_far(lhs, bias, skip, state, pieces):
+    shape = state[0].shape
+    return pl.pallas_call(
+        functools.partial(far_kernel, skip),
+        out_shape=jax.ShapeDtypeStruct(shape, jnp.bfloat16),
+        in_specs=[VMEM, VMEM, ANY, VMEM, VMEM] + [VMEM] * len(pieces),
+        out_specs=ANY,
+        scratch_shapes=stage_shapes(shape),
+        input_output_aliases={2: 0},
+        compiler_params=PARAMS,
+        name="far",
+    )(lhs, bias, *state, *pieces)
+
+
+def attend_exchanged(queries, block, lengths):
     def swap(array, code):
         return lax.ppermute(array, "ctx", [(i, i ^ code) for i in range(8)])
 
-    crossed = swap(block, far)
+    crossed = swap(block, 6)
     near = [swap(block, code) for code in (2, 1, 3)]
-    crossed_near = [swap(crossed, code) for code in (2, 1, 3)]
-    codes = (0, 2, 1, 3, far, far ^ 2, far ^ 1, far ^ 3)
-    return [block, *near, crossed, *crossed_near], codes
+    lhs, bias = make_ready(queries, (0, 2, 1, 3, 6, 4, 7, 5), lengths)
+    crossed, lhs = lax.optimization_barrier((crossed, lhs))
+    spread = [swap(crossed, code) for code in (2, 1, 3)]
+    state = attend_near(queries.shape, lhs, bias, [block, *near, crossed])
+    return attend_far(lhs, bias, 5, state, spread)
 
 
 def stream_kernel(step, lengths, query_ref, block_ref, out_ref, peak_ref, both_ref):
@@ -153,8 +292,7 @@
     block = jnp.stack([keys, values]).transpose(0, 2, 1, 3)
     if ctx != 8:
         return attend_gathered(queries, lax.all_gather(block, "ctx"), seq_lengths)
-    pieces, codes = exchange(block, 6)
-    return attend_pieces(queries, pieces, codes, seq_lengths)
+    return attend_exchanged(queries, block, seq_lengths)
 
 
 def solution(mesh):

time: 25.9 us -> 22.1 us (0.85)
  waiting for transfers between devices: 6.2 us -> 3.37 us
  Pallas kernels: 4.61 us -> 3.54 us
    ppermute x7, waiting for transfers between devices: 6.2 us -> 3.37 us  [swap(): return lax.ppermute(array, 'ctx', [(i, i ^ code) for i in range(8)])]
    pallas_call x1 -> x3, Pallas kernels: 4.61 us -> 3.54 us  [the longest x1 2.3 us: attend_near(): pl.pallas_call(near_kernel, out_shape=(jax.ShapeDtypeStruct(shape, jnp.bf...]
  transfers between devices with their start and end apart: 7 -> 7, of which waited for: 6 -> 2; matrix products, arithmetic and copies ran while one was open for 0% -> 0% of each run, Pallas kernels for 0% -> 16%
where the time goes in v2:
time: 22.1 us; the launch traced here: 21.9 us
  starting transfers between devices  14.1 us (64%)
  Pallas kernels  3.54 us (16%)
  waiting for transfers between devices  3.37 us (15%)
  local copies, waits for them, and re-layouts  0.89 us (4%)
    ppermute x7, starting transfers between devices, swap(): return lax.ppermute(array, 'ctx', [(i, i ^ code) for i in range(8)])  14.1 us
    ppermute x7, waiting for transfers between devices, swap(): return lax.ppermute(array, 'ctx', [(i, i ^ code) for i in range(8)])  3.37 us
    pallas_call x1, Pallas kernels, attend_near(): pl.pallas_call(near_kernel, out_shape=(jax.ShapeDtypeStruct(shape, jnp.bf...  2.3 us
    pallas_call x1, Pallas kernels, make_ready(): pl.pallas_call(functools.partial(ready_kernel, codes), out_shape=(jax.Sha...  1.15 us
    another operation x1, local copies, waits for them, and re-layouts, on_device(): block = jnp.stack([keys, values]).transpose(0, 2, 1, 3)  0.89 us
  transfers between devices with their start and end apart: 7, of which 2 were waited for; matrix products, arithmetic and copies ran while one was open for 0% of the time, Pallas kernels for 16%

profile of v2, /device:TPU:0, one launch (start us, length us, event | category | flops | bytes accessed | tf_op | source)
XLA Modules:
  0.0 21.9 jit_solution(14806874447852615524)
XLA Ops:
  0.0 0.9 %copy_bitcast_fusion = (bf16[1,128,2,128]{3,1,2,0:T(8,128)(2,1)S(1)}, bf16[1,128,2,128]{3,1,2,0:T(8,128)(2,1)S(1)}) fusion(bf16[128,2,128]{2,1,0:T(2,128)(2,1)} %param.6, bf16[128,2,128]{2,1,0:T(2,128)(2,1)} %param.5), kind=kLoop, calls=%fused_computation.1 | loop fusion | bytes 262144 | tf_op jit(solution)/shard_map/stack | solution.py:292
  0.9 5.1 %collective-permute-start = (bf16[2,2,128,128]{3,2,1,0:T(8,128)(2,1)S(1)}, bf16[2,2,128,128]{3,2,1,0:T(8,128)(2,1)S(1)}, u32[]{:S(2)}, u32[]{:S(2)}) collective-permute-start(bf16[2,2,128,128]{3,2,1,0:T(8,128)(2,1)S(1)} %maximum_bitcast_fusion.refs_0_), channel_id=1, source_target_pairs={{0,12},{2,14},{4,8},{6,10},{8,4},{10,6},{12,0},{14,2},{1,13},{3,15... | collective-permute-start | bytes 393224 | tf_op jit(solution)/shard_map/ppermute | solution.py:209
  6.0 0.0 collective-permute-start.1
  6.0 1.5 %collective-permute-start.2 = (bf16[2,2,128,128]{3,2,1,0:T(8,128)(2,1)S(1)}, bf16[2,2,128,128]{3,2,1,0:T(8,128)(2,1)S(1)}, u32[]{:S(2)}, u32[]{:S(2)}) collective-permute-start(bf16[2,2,128,128]{3,2,1,0:T(8,128)(2,1)S(1)} %maximum_bitcast_fusion.refs_0_), channel_id=1, source_target_pairs={{0,2},{2,0},{4,6},{6,4},{8,10},{10,8},{12,14},{14,12},{1,3},{3,1},... | collective-permute-start | bytes 393224 | tf_op jit(solution)/shard_map/ppermute | solution.py:209
  7.5 2.0 %collective-permute-start.3 = (bf16[2,2,128,128]{3,2,1,0:T(8,128)(2,1)S(1)}, bf16[2,2,128,128]{3,2,1,0:T(8,128)(2,1)S(1)}, u32[]{:S(2)}, u32[]{:S(2)}) collective-permute-start(bf16[2,2,128,128]{3,2,1,0:T(8,128)(2,1)S(1)} %maximum_bitcast_fusion.refs_0_), channel_id=1, source_target_pairs={{0,6},{2,4},{4,2},{6,0},{8,14},{10,12},{12,10},{14,8},{1,7},{3,5},... | collective-permute-start | bytes 393224 | tf_op jit(solution)/shard_map/ppermute | solution.py:209
  9.5 1.1 %ready.1 = (bf16[2,1024,256]{2,1,0:T(8,128)(2,1)S(1)}, bf16[8,128,128]{2,1,0:T(8,128)(2,1)S(1)}) custom-call(s32[4]{0:T(128)} %lengths_hbm.1, bf16[128,2,8,128]{3,2,1,0:T(8,128)(2,1)} %query_hbm.1), custom_call_target="tpu_custom_call" | custom-call | tf_op jit(solution)/shard_map/ready/pallas_call | solution.py:154
  10.7 0.0 collective-permute-done.refs_4_
  10.7 1.4 %collective-permute-start.4 = (bf16[2,2,128,128]{3,2,1,0:T(8,128)(2,1)S(1)}, bf16[2,2,128,128]{3,2,1,0:T(8,128)(2,1)S(1)}, u32[]{:S(2)}, u32[]{:S(2)}) collective-permute-start(bf16[2,2,128,128]{3,2,1,0:T(8,128)(2,1)S(1)} %collective-permute-done.refs_4_), channel_id=1, source_target_pairs={{0,4},{2,6},{4,0},{6,2},{8,12},{10,14},{12,8},{14,10},{1,5},{3,7},... | collective-permute-start | bytes 393224 | tf_op jit(solution)/shard_map/ppermute | solution.py:209
  12.1 1.5 %collective-permute-start.5 = (bf16[2,2,128,128]{3,2,1,0:T(8,128)(2,1)S(1)}, bf16[2,2,128,128]{3,2,1,0:T(8,128)(2,1)S(1)}, u32[]{:S(2)}, u32[]{:S(2)}) collective-permute-start(bf16[2,2,128,128]{3,2,1,0:T(8,128)(2,1)S(1)} %collective-permute-done.refs_4_), channel_id=1, source_target_pairs={{0,2},{2,0},{4,6},{6,4},{8,10},{10,8},{12,14},{14,12},{1,3},{3,1},... | collective-permute-start | bytes 393224 | tf_op jit(solution)/shard_map/ppermute | solution.py:209
  13.5 0.0 collective-permute-done.1.refs_1_
  13.5 2.6 %collective-permute-start.6 = (bf16[2,2,128,128]{3,2,1,0:T(8,128)(2,1)S(1)}, bf16[2,2,128,128]{3,2,1,0:T(8,128)(2,1)S(1)}, u32[]{:S(2)}, u32[]{:S(2)}) collective-permute-start(bf16[2,2,128,128]{3,2,1,0:T(8,128)(2,1)S(1)} %collective-permute-done.refs_4_), channel_id=1, source_target_pairs={{0,6},{2,4},{4,2},{6,0},{8,14},{10,12},{12,10},{14,8},{1,7},{3,5},... | collective-permute-start | bytes 393224 | tf_op jit(solution)/shard_map/ppermute | solution.py:209
  16.2 0.0 collective-permute-done.2.refs_2_
  16.2 0.6 %collective-permute-done.3.refs_3_ = bf16[2,2,128,128]{3,2,1,0:T(8,128)(2,1)S(1)} collective-permute-done((bf16[2,2,128,128]{3,2,1,0:T(8,128)(2,1)S(1)}, bf16[2,2,128,128]{3,2,1,0:T(8,128)(2,1)S(1)}, u32[]{:S(2)}, u32[]{:S(2)}) %collective-permute-start.3) | collective-permute-done | bytes 131104 | tf_op jit(solution)/shard_map/ppermute | solution.py:209
  16.7 2.3 %near.1 = (bf16[128,2,8,128]{3,2,1,0:T(8,128)(2,1)}, f32[2,1024,128]{2,1,0:T(8,128)S(1)}, f32[2,1024,256]{2,1,0:T(8,128)S(1)}) custom-call(bf16[2,1024,256]{2,1,0:T(8,128)(2,1)S(1)} %get-tuple-element.13.lhs_ref, bf16[8,128,128]{2,1,0:T(8,128)(2,1)S(1)} %get-tuple-element.14.bias_ref, bf16[2,2,128,128]{3,2,1,0:T(8,128)(2,1)S(1)} %maximum_bitcast_fusion.refs_0_, ...), custom_call_target="tpu_custom_call" | custom-call | tf_op jit(solution)/shard_map/near/pallas_call | solution.py:178
  19.0 0.0 collective-permute-done.4.refs_0_
  19.1 0.0 collective-permute-done.5.refs_1_
  19.1 2.7 %collective-permute-done.6.refs_2_ = bf16[2,2,128,128]{3,2,1,0:T(8,128)(2,1)S(1)} collective-permute-done((bf16[2,2,128,128]{3,2,1,0:T(8,128)(2,1)S(1)}, bf16[2,2,128,128]{3,2,1,0:T(8,128)(2,1)S(1)}, u32[]{:S(2)}, u32[]{:S(2)}) %collective-permute-start.6) | collective-permute-done | bytes 131104 | tf_op jit(solution)/shard_map/ppermute | solution.py:209
  21.8 0.1 far.1
  (1 shorter events, 0.0 us)
Async XLA Ops:
  0.9 9.8 %collective-permute-start = (bf16[2,2,128,128]{3,2,1,0:T(8,128)(2,1)S(1)}, bf16[2,2,128,128]{3,2,1,0:T(8,128)(2,1)S(1)}, u32[]{:S(2)}, u32[]{:S(2)}) collective-permute-start(bf16[2,2,128,128]{3,2,1,0:T(8,128)(2,1)S(1)} %maximum_bitcast_fusion.refs_0_), channel_id=1, source_target_pairs={{0,12},{2,14},{4,8},{6,10},{8,4},{10,6},{12,0},{14,2},{1,13},{3,15... | collective-permute-start | bytes 393224 | tf_op jit(solution)/shard_map/ppermute | solution.py:209
  6.0 7.5 %collective-permute-start.1 = (bf16[2,2,128,128]{3,2,1,0:T(8,128)(2,1)S(1)}, bf16[2,2,128,128]{3,2,1,0:T(8,128)(2,1)S(1)}, u32[]{:S(2)}, u32[]{:S(2)}) collective-permute-start(bf16[2,2,128,128]{3,2,1,0:T(8,128)(2,1)S(1)} %maximum_bitcast_fusion.refs_0_), channel_id=1, source_target_pairs={{0,4},{2,6},{4,0},{6,2},{8,12},{10,14},{12,8},{14,10},{1,5},{3,7},... | collective-permute-start | bytes 393224 | tf_op jit(solution)/shard_map/ppermute | solution.py:209
  6.0 10.1 %collective-permute-start.2 = (bf16[2,2,128,128]{3,2,1,0:T(8,128)(2,1)S(1)}, bf16[2,2,128,128]{3,2,1,0:T(8,128)(2,1)S(1)}, u32[]{:S(2)}, u32[]{:S(2)}) collective-permute-start(bf16[2,2,128,128]{3,2,1,0:T(8,128)(2,1)S(1)} %maximum_bitcast_fusion.refs_0_), channel_id=1, source_target_pairs={{0,2},{2,0},{4,6},{6,4},{8,10},{10,8},{12,14},{14,12},{1,3},{3,1},... | collective-permute-start | bytes 393224 | tf_op jit(solution)/shard_map/ppermute | solution.py:209
  7.5 9.2 %collective-permute-start.3 = (bf16[2,2,128,128]{3,2,1,0:T(8,128)(2,1)S(1)}, bf16[2,2,128,128]{3,2,1,0:T(8,128)(2,1)S(1)}, u32[]{:S(2)}, u32[]{:S(2)}) collective-permute-start(bf16[2,2,128,128]{3,2,1,0:T(8,128)(2,1)S(1)} %maximum_bitcast_fusion.refs_0_), channel_id=1, source_target_pairs={{0,6},{2,4},{4,2},{6,0},{8,14},{10,12},{12,10},{14,8},{1,7},{3,5},... | collective-permute-start | bytes 393224 | tf_op jit(solution)/shard_map/ppermute | solution.py:209
  10.7 8.4 %collective-permute-start.4 = (bf16[2,2,128,128]{3,2,1,0:T(8,128)(2,1)S(1)}, bf16[2,2,128,128]{3,2,1,0:T(8,128)(2,1)S(1)}, u32[]{:S(2)}, u32[]{:S(2)}) collective-permute-start(bf16[2,2,128,128]{3,2,1,0:T(8,128)(2,1)S(1)} %collective-permute-done.refs_4_), channel_id=1, source_target_pairs={{0,4},{2,6},{4,0},{6,2},{8,12},{10,14},{12,8},{14,10},{1,5},{3,7},... | collective-permute-start | bytes 393224 | tf_op jit(solution)/shard_map/ppermute | solution.py:209
  12.1 7.0 %collective-permute-start.5 = (bf16[2,2,128,128]{3,2,1,0:T(8,128)(2,1)S(1)}, bf16[2,2,128,128]{3,2,1,0:T(8,128)(2,1)S(1)}, u32[]{:S(2)}, u32[]{:S(2)}) collective-permute-start(bf16[2,2,128,128]{3,2,1,0:T(8,128)(2,1)S(1)} %collective-permute-done.refs_4_), channel_id=1, source_target_pairs={{0,2},{2,0},{4,6},{6,4},{8,10},{10,8},{12,14},{14,12},{1,3},{3,1},... | collective-permute-start | bytes 393224 | tf_op jit(solution)/shard_map/ppermute | solution.py:209
  13.5 8.3 %collective-permute-start.6 = (bf16[2,2,128,128]{3,2,1,0:T(8,128)(2,1)S(1)}, bf16[2,2,128,128]{3,2,1,0:T(8,128)(2,1)S(1)}, u32[]{:S(2)}, u32[]{:S(2)}) collective-permute-start(bf16[2,2,128,128]{3,2,1,0:T(8,128)(2,1)S(1)} %collective-permute-done.refs_4_), channel_id=1, source_target_pairs={{0,6},{2,4},{4,2},{6,0},{8,14},{10,12},{12,10},{14,8},{1,7},{3,5},... | collective-permute-start | bytes 393224 | tf_op jit(solution)/shard_map/ppermute | solution.py:209

commit v3 on v2

--- a/solution.py
+++ b/solution.py
@@ -11,6 +11,8 @@
 MASKED = -1e30
 ROW_TILE = 256
 HEADROOM = 60.0
+NEAR = (3, 2, 1)
+SPREAD = (3, 2, 1)
 
 
 def key_bias(lengths, own, block, rows):
@@ -59,11 +61,34 @@
     return jnp.dot(weights, right, preferred_element_type=jnp.float32)
 
 
+class State:
+    def __init__(self, peak_ref, both_ref):
+        self.peak, self.both = peak_ref, both_ref
+
+    def restart(self):
+        pass
+
+    def wait(self):
+        pass
+
+    def __call__(self, h, first, peak, both):
+        rows = pl.ds(first, both.shape[0])
+        self.peak[h, rows] = jnp.broadcast_to(peak, (both.shape[0], self.peak.shape[-1]))
+        self.both[h, rows] = both
+
+
 class Output:
     def __init__(self, out_ref, stage_ref, semaphores):
         self.out, self.stage, self.semaphores, self.copies = out_ref, stage_ref, semaphores, []
 
-    def put(self, h, first, both):
+    def restart(self):
+        self.copies = []
+
+    def wait(self):
+        for copy in self.copies:
+            copy.wait()
+
+    def __call__(self, h, first, peak, both):
         _, _, group, size = self.stage.shape
         result = both[:, :size] / both[:, size:]
         queries = pl.ds(first // group, result.shape[0] // group)
@@ -74,10 +99,6 @@
         copy.start()
         self.copies.append(copy)
 
-    def wait(self):
-        for copy in self.copies:
-            copy.wait()
-
 
 def tiles_of(lhs_ref):
     heads, rows, _ = lhs_ref.shape
@@ -92,55 +113,65 @@
     upper = lax.axis_index("ctx") >= 4
     biases = [bias_ref[n] for n in range(len(pieces))]
 
+    def attend(members, put):
+        for h, first, tile in tiles_of(lhs_ref):
+            scores = scores_of(lhs_ref[h, pl.ds(first, tile)], h, members, biases)
+            peak = jnp.max(scores, axis=1, keepdims=True)
+            put(h, first, peak, weigh((scores - peak) * scale, h, members))
+        put.wait()
+
     @pl.when(upper)
     def _():
-        for h, first, tile in tiles_of(lhs_ref):
-            scores = scores_of(lhs_ref[h, pl.ds(first, tile)], h, pieces, biases)
-            peak = jnp.max(scores, axis=1, keepdims=True)
-            peak_ref[h, pl.ds(first, tile)] = jnp.broadcast_to(peak, (tile, size))
-            both_ref[h, pl.ds(first, tile)] = weigh((scores - peak) * scale, h, pieces)
+        attend(pieces, State(peak_ref, both_ref))
 
     @pl.when(jnp.logical_not(upper))
     def _():
-        output = Output(out_ref, stage_ref, semaphores)
-        for h, first, tile in tiles_of(lhs_ref):
-            scores = scores_of(lhs_ref[h, pl.ds(first, tile)], h, pieces[:4], biases)
-            peak = jnp.max(scores, axis=1, keepdims=True)
-            output.put(h, first, weigh((scores - peak) * scale, h, pieces[:4]))
-        output.wait()
-
-
-def far_kernel(skip, lhs_ref, bias_ref, _, peak_ref, both_ref, *refs):
-    pieces, (out_ref, stage_ref, semaphores) = refs[:-3], refs[-3:]
-    size = stage_ref.shape[-1]
+        attend(pieces[:4], Output(out_ref, stage_ref, semaphores))
+
+
+def fold(lhs_ref, peak_ref, both_ref, pieces, biases, put):
+    size = peak_ref.shape[-1]
     scale = math.log2(math.e) / math.sqrt(size)
-    biases = [bias_ref[skip + n] for n in range(len(pieces))]
-
-    @pl.when(lax.axis_index("ctx") >= 4)
-    def _():
-        output = Output(out_ref, stage_ref, semaphores)
-        most = jnp.full((1, 1), MASKED, jnp.float32)
+    most = jnp.full((1, 1), MASKED, jnp.float32)
+    for h, first, tile in tiles_of(lhs_ref):
+        rows = pl.ds(first, tile)
+        before = peak_ref[h, rows]
+        scores = scores_of(lhs_ref[h, rows], h, pieces, biases)
+        above = (scores - jnp.concatenate([before] * len(pieces), axis=1)) * scale
+        most = jnp.maximum(most, jnp.max(above, axis=0, keepdims=True))
+        put(h, first, before, both_ref[h, rows] + weigh(above, h, pieces))
+    put.wait()
+
+    @pl.when(jnp.max(most) > HEADROOM)
+    def _():
+        put.restart()
         for h, first, tile in tiles_of(lhs_ref):
             rows = pl.ds(first, tile)
             scores = scores_of(lhs_ref[h, rows], h, pieces, biases)
             before = peak_ref[h, rows]
-            above = (scores - jnp.concatenate([before] * len(pieces), axis=1)) * scale
-            most = jnp.maximum(most, jnp.max(above, axis=0, keepdims=True))
-            output.put(h, first, both_ref[h, rows] + weigh(above, h, pieces))
-        output.wait()
-
-        @pl.when(jnp.max(most) > HEADROOM)
-        def _():
-            output = Output(out_ref, stage_ref, semaphores)
-            for h, first, tile in tiles_of(lhs_ref):
-                rows = pl.ds(first, tile)
-                scores = scores_of(lhs_ref[h, rows], h, pieces, biases)
-                before = peak_ref[h, rows]
-                peak = jnp.maximum(before, jnp.max(scores, axis=1, keepdims=True))
-                fade = jnp.exp2((before - peak) * scale)
-                added = weigh((scores - peak[:, :1]) * scale, h, pieces)
-                output.put(h, first, both_ref[h, rows] * jnp.concatenate([fade, fade], axis=1) + added)
-            output.wait()
+            peak = jnp.maximum(before, jnp.max(scores, axis=1, keepdims=True))
+            fade = jnp.exp2((before - peak) * scale)
+            added = weigh((scores - jnp.concatenate([peak] * len(pieces), axis=1)) * scale, h, pieces)
+            put(h, first, peak, both_ref[h, rows] * jnp.concatenate([fade, fade], axis=1) + added)
+        put.wait()
+
+
+def middle_kernel(skip, lhs_ref, bias_ref, peak_ref, both_ref, *refs):
+    pieces, (peak_out, both_out) = refs[:-2], refs[-2:]
+    biases = [bias_ref[skip + n] for n in range(len(pieces))]
+
+    @pl.when(lax.axis_index("ctx") >= 4)
+    def _():
+        fold(lhs_ref, peak_ref, both_ref, pieces, biases, State(peak_out, both_out))
+
+
+def far_kernel(skip, lhs_ref, bias_ref, _, peak_ref, both_ref, *refs):
+    pieces, (out_ref, stage_ref, semaphores) = refs[:-3], refs[-3:]
+    biases = [bias_ref[skip + n] for n in range(len(pieces))]
+
+    @pl.when(lax.axis_index("ctx") >= 4)
+    def _():
+        fold(lhs_ref, peak_ref, both_ref, pieces, biases, Output(out_ref, stage_ref, semaphores))
 
 
 VMEM = pl.BlockSpec(memory_space=pltpu.VMEM)
@@ -190,6 +221,19 @@
     )(lhs, bias, *pieces)
 
 
+def attend_middle(lhs, bias, skip, state, pieces):
+    out, peak, both = state
+    peak, both = pl.pallas_call(
+        functools.partial(middle_kernel, skip),
+        out_shape=(jax.ShapeDtypeStruct(peak.shape, peak.dtype), jax.ShapeDtypeStruct(both.shape, both.dtype)),
+        in_specs=[VMEM] * (4 + len(pieces)),
+        out_specs=(VMEM, VMEM),
+        compiler_params=PARAMS,
+        name="middle",
+    )(lhs, bias, peak, both, *pieces)
+    return out, peak, both
+
+
 def attend_far(lhs, bias, skip, state, pieces):
     shape = state[0].shape
     return pl.pallas_call(
@@ -205,16 +249,17 @@
 
 
 def attend_exchanged(queries, block, lengths):
-    def swap(array, code):
-        return lax.ppermute(array, "ctx", [(i, i ^ code) for i in range(8)])
+    def swap(array, code, members=range(8)):
+        return lax.ppermute(array, "ctx", [(i, i ^ code) for i in members])
 
     crossed = swap(block, 6)
-    near = [swap(block, code) for code in (2, 1, 3)]
-    lhs, bias = make_ready(queries, (0, 2, 1, 3, 6, 4, 7, 5), lengths)
+    near = [swap(block, code) for code in NEAR]
+    lhs, bias = make_ready(queries, (0, *NEAR, 6, *[6 ^ code for code in SPREAD]), lengths)
     crossed, lhs = lax.optimization_barrier((crossed, lhs))
-    spread = [swap(crossed, code) for code in (2, 1, 3)]
+    spread = [swap(crossed, code, range(4, 8) if code == 3 else range(8)) for code in SPREAD]
     state = attend_near(queries.shape, lhs, bias, [block, *near, crossed])
-    return attend_far(lhs, bias, 5, state, spread)
+    state = attend_middle(lhs, bias, 5, state, spread[:1])
+    return attend_far(lhs, bias, 6, state, spread[1:])
 
 
 def stream_kernel(step, lengths, query_ref, block_ref, out_ref, peak_ref, both_ref):

time: 22.1 us -> 21.1 us (0.955)
  the two profiles are of different devices: /device:TPU:0 before, /device:TPU:24 now
where the time goes in v3:
time: 21.1 us; the launch traced here: 20.9 us
  starting transfers between devices  9.08 us (43%)
  Pallas kernels  6.21 us (29%)
  waiting for transfers between devices  4.62 us (22%)
  local copies, waits for them, and re-layouts  0.89 us (4%)
    ppermute x7, starting transfers between devices, swap(): return lax.ppermute(array, 'ctx', [(i, i ^ code) for i in members])  9.08 us
    ppermute x7, waiting for transfers between devices, swap(): return lax.ppermute(array, 'ctx', [(i, i ^ code) for i in members])  4.62 us
    pallas_call x1, Pallas kernels, attend_near(): pl.pallas_call(near_kernel, out_shape=(jax.ShapeDtypeStruct(shape, jnp.bf...  2.3 us
    pallas_call x1, Pallas kernels, attend_far(): pl.pallas_call(functools.partial(far_kernel, skip), out_shape=jax.ShapeDt...  1.81 us
    pallas_call x1, Pallas kernels, make_ready(): pl.pallas_call(functools.partial(ready_kernel, codes), out_shape=(jax.Sha...  1.15 us
    pallas_call x1, Pallas kernels, attend_middle(): pl.pallas_call(functools.partial(middle_kernel, skip), out_shape=(jax.Sha...  0.96 us
    another operation x1, local copies, waits for them, and re-layouts, on_device(): block = jnp.stack([keys, values]).transpose(0, 2, 1, 3)  0.89 us
  transfers between devices with their start and end apart: 7, of which 4 were waited for; matrix products, arithmetic and copies ran while one was open for 0% of the time, Pallas kernels for 21%

profile of v3, /device:TPU:24, one launch (start us, length us, event | category | flops | bytes accessed | tf_op | source)
XLA Modules:
  0.0 20.9 jit_solution(8804777700224941814)
XLA Ops:
  0.0 0.9 %copy_bitcast_fusion = (bf16[1,128,2,128]{3,1,2,0:T(8,128)(2,1)S(1)}, bf16[1,128,2,128]{3,1,2,0:T(8,128)(2,1)S(1)}) fusion(bf16[128,2,128]{2,1,0:T(2,128)(2,1)} %param.6, bf16[128,2,128]{2,1,0:T(2,128)(2,1)} %param.5), kind=kLoop, calls=%fused_computation.1 | loop fusion | bytes 262144 | tf_op jit(solution)/shard_map/stack | solution.py:337
  0.9 0.1 collective-permute-start
  1.0 1.8 %collective-permute-start.1 = (bf16[2,2,128,128]{3,2,1,0:T(8,128)(2,1)S(1)}, bf16[2,2,128,128]{3,2,1,0:T(8,128)(2,1)S(1)}, u32[]{:S(2)}, u32[]{:S(2)}) collective-permute-start(bf16[2,2,128,128]{3,2,1,0:T(8,128)(2,1)S(1)} %maximum_bitcast_fusion.refs_0_), channel_id=1, source_target_pairs={{0,6},{2,4},{4,2},{6,0},{8,14},{10,12},{12,10},{14,8},{1,7},{3,5},... | collective-permute-start | bytes 393224 | tf_op jit(solution)/shard_map/ppermute | solution.py:253
  2.8 1.3 %collective-permute-start.2 = (bf16[2,2,128,128]{3,2,1,0:T(8,128)(2,1)S(1)}, bf16[2,2,128,128]{3,2,1,0:T(8,128)(2,1)S(1)}, u32[]{:S(2)}, u32[]{:S(2)}) collective-permute-start(bf16[2,2,128,128]{3,2,1,0:T(8,128)(2,1)S(1)} %maximum_bitcast_fusion.refs_0_), channel_id=1, source_target_pairs={{0,4},{2,6},{4,0},{6,2},{8,12},{10,14},{12,8},{14,10},{1,5},{3,7},... | collective-permute-start | bytes 393224 | tf_op jit(solution)/shard_map/ppermute | solution.py:253
  4.2 0.4 %collective-permute-start.3 = (bf16[2,2,128,128]{3,2,1,0:T(8,128)(2,1)S(1)}, bf16[2,2,128,128]{3,2,1,0:T(8,128)(2,1)S(1)}, u32[]{:S(2)}, u32[]{:S(2)}) collective-permute-start(bf16[2,2,128,128]{3,2,1,0:T(8,128)(2,1)S(1)} %maximum_bitcast_fusion.refs_0_), channel_id=1, source_target_pairs={{0,2},{2,0},{4,6},{6,4},{8,10},{10,8},{12,14},{14,12},{1,3},{3,1},... | collective-permute-start | bytes 393224 | tf_op jit(solution)/shard_map/ppermute | solution.py:253
  4.6 1.1 %ready.1 = (bf16[2,1024,256]{2,1,0:T(8,128)(2,1)S(1)}, bf16[8,128,128]{2,1,0:T(8,128)(2,1)S(1)}) custom-call(s32[4]{0:T(128)} %lengths_hbm.1, bf16[128,2,8,128]{3,2,1,0:T(8,128)(2,1)} %query_hbm.1), custom_call_target="tpu_custom_call" | custom-call | tf_op jit(solution)/shard_map/ready/pallas_call | solution.py:185
  5.7 3.5 %collective-permute-done.refs_4_ = bf16[2,2,128,128]{3,2,1,0:T(8,128)(2,1)S(1)} collective-permute-done((bf16[2,2,128,128]{3,2,1,0:T(8,128)(2,1)S(1)}, bf16[2,2,128,128]{3,2,1,0:T(8,128)(2,1)S(1)}, u32[]{:S(2)}, u32[]{:S(2)}) %collective-permute-start) | collective-permute-done | bytes 131104 | tf_op jit(solution)/shard_map/ppermute | solution.py:253
  9.2 2.9 %collective-permute-start.4 = (bf16[2,2,128,128]{3,2,1,0:T(8,128)(2,1)S(1)}, bf16[2,2,128,128]{3,2,1,0:T(8,128)(2,1)S(1)}, u32[]{:S(2)}, u32[]{:S(2)}) collective-permute-start(bf16[2,2,128,128]{3,2,1,0:T(8,128)(2,1)S(1)} %collective-permute-done.refs_4_), channel_id=1, source_target_pairs={{8,14},{10,12},{12,10},{14,8},{9,15},{11,13},{13,11},{15,9},{24,30... | collective-permute-start | bytes 393224 | tf_op jit(solution)/shard_map/ppermute | solution.py:253
  12.1 2.0 %collective-permute-start.5 = (bf16[2,2,128,128]{3,2,1,0:T(8,128)(2,1)S(1)}, bf16[2,2,128,128]{3,2,1,0:T(8,128)(2,1)S(1)}, u32[]{:S(2)}, u32[]{:S(2)}) collective-permute-start(bf16[2,2,128,128]{3,2,1,0:T(8,128)(2,1)S(1)} %collective-permute-done.refs_4_), channel_id=1, source_target_pairs={{0,4},{2,6},{4,0},{6,2},{8,12},{10,14},{12,8},{14,10},{1,5},{3,7},... | collective-permute-start | bytes 393224 | tf_op jit(solution)/shard_map/ppermute | solution.py:253
  14.1 0.0 collective-permute-done.1.refs_1_
  14.1 0.5 %collective-permute-start.6 = (bf16[2,2,128,128]{3,2,1,0:T(8,128)(2,1)S(1)}, bf16[2,2,128,128]{3,2,1,0:T(8,128)(2,1)S(1)}, u32[]{:S(2)}, u32[]{:S(2)}) collective-permute-start(bf16[2,2,128,128]{3,2,1,0:T(8,128)(2,1)S(1)} %collective-permute-done.refs_4_), channel_id=1, source_target_pairs={{0,2},{2,0},{4,6},{6,4},{8,10},{10,8},{12,14},{14,12},{1,3},{3,1},... | collective-permute-start | bytes 393224 | tf_op jit(solution)/shard_map/ppermute | solution.py:253
  14.6 0.0 collective-permute-done.2.refs_2_
  14.6 0.0 collective-permute-done.3.refs_3_
  14.6 2.3 %near.1 = (bf16[128,2,8,128]{3,2,1,0:T(8,128)(2,1)}, f32[2,1024,128]{2,1,0:T(8,128)S(1)}, f32[2,1024,256]{2,1,0:T(8,128)S(1)}) custom-call(bf16[2,1024,256]{2,1,0:T(8,128)(2,1)S(1)} %get-tuple-element.15.lhs_ref, bf16[8,128,128]{2,1,0:T(8,128)(2,1)S(1)} %get-tuple-element.16.bias_ref, bf16[2,2,128,128]{3,2,1,0:T(8,128)(2,1)S(1)} %maximum_bitcast_fusion.refs_0_, ...), custom_call_target="tpu_custom_call" | custom-call | tf_op jit(solution)/shard_map/near/pallas_call | solution.py:209
  16.9 0.1 collective-permute-done.4.refs_0_
  17.0 1.0 %middle.1 = (f32[2,1024,128]{2,1,0:T(8,128)S(1)}, f32[2,1024,256]{2,1,0:T(8,128)S(1)}) custom-call(bf16[2,1024,256]{2,1,0:T(8,128)(2,1)S(1)} %get-tuple-element.15.lhs_ref, bf16[8,128,128]{2,1,0:T(8,128)(2,1)S(1)} %get-tuple-element.16.bias_ref, f32[2,1024,128]{2,1,0:T(8,128)S(1)} %get-tuple-element.19.peak_ref, ...), custom_call_target="tpu_custom_call" | custom-call | tf_op jit(solution)/shard_map/middle/pallas_call | solution.py:226
  18.0 0.5 %collective-permute-done.5.refs_0_ = bf16[2,2,128,128]{3,2,1,0:T(8,128)(2,1)S(1)} collective-permute-done((bf16[2,2,128,128]{3,2,1,0:T(8,128)(2,1)S(1)}, bf16[2,2,128,128]{3,2,1,0:T(8,128)(2,1)S(1)}, u32[]{:S(2)}, u32[]{:S(2)}) %collective-permute-start.5) | collective-permute-done | bytes 131104 | tf_op jit(solution)/shard_map/ppermute | solution.py:253
  18.5 0.6 %collective-permute-done.6.refs_1_ = bf16[2,2,128,128]{3,2,1,0:T(8,128)(2,1)S(1)} collective-permute-done((bf16[2,2,128,128]{3,2,1,0:T(8,128)(2,1)S(1)}, bf16[2,2,128,128]{3,2,1,0:T(8,128)(2,1)S(1)}, u32[]{:S(2)}, u32[]{:S(2)}) %collective-permute-start.6) | collective-permute-done | bytes 131104 | tf_op jit(solution)/shard_map/ppermute | solution.py:253
  19.1 1.8 %far.1 = bf16[128,2,8,128]{3,2,1,0:T(8,128)(2,1)} custom-call(bf16[2,1024,256]{2,1,0:T(8,128)(2,1)S(1)} %get-tuple-element.15.lhs_ref, bf16[8,128,128]{2,1,0:T(8,128)(2,1)S(1)} %get-tuple-element.16.bias_ref, bf16[128,2,8,128]{3,2,1,0:T(8,128)(2,1)} %get-tuple-element.18._, ...), custom_call_target="tpu_custom_call", output_to_operand_aliasing={{}: (2, {})} | custom-call | tf_op jit(solution)/shard_map/far/pallas_call | solution.py:239
  (1 shorter events, 0.0 us)
Async XLA Ops:
  0.9 8.3 %collective-permute-start = (bf16[2,2,128,128]{3,2,1,0:T(8,128)(2,1)S(1)}, bf16[2,2,128,128]{3,2,1,0:T(8,128)(2,1)S(1)}, u32[]{:S(2)}, u32[]{:S(2)}) collective-permute-start(bf16[2,2,128,128]{3,2,1,0:T(8,128)(2,1)S(1)} %maximum_bitcast_fusion.refs_0_), channel_id=1, source_target_pairs={{0,12},{2,14},{4,8},{6,10},{8,4},{10,6},{12,0},{14,2},{1,13},{3,15... | collective-permute-start | bytes 393224 | tf_op jit(solution)/shard_map/ppermute | solution.py:253
  1.0 13.1 %collective-permute-start.1 = (bf16[2,2,128,128]{3,2,1,0:T(8,128)(2,1)S(1)}, bf16[2,2,128,128]{3,2,1,0:T(8,128)(2,1)S(1)}, u32[]{:S(2)}, u32[]{:S(2)}) collective-permute-start(bf16[2,2,128,128]{3,2,1,0:T(8,128)(2,1)S(1)} %maximum_bitcast_fusion.refs_0_), channel_id=1, source_target_pairs={{0,6},{2,4},{4,2},{6,0},{8,14},{10,12},{12,10},{14,8},{1,7},{3,5},... | collective-permute-start | bytes 393224 | tf_op jit(solution)/shard_map/ppermute | solution.py:253
  2.8 11.8 %collective-permute-start.2 = (bf16[2,2,128,128]{3,2,1,0:T(8,128)(2,1)S(1)}, bf16[2,2,128,128]{3,2,1,0:T(8,128)(2,1)S(1)}, u32[]{:S(2)}, u32[]{:S(2)}) collective-permute-start(bf16[2,2,128,128]{3,2,1,0:T(8,128)(2,1)S(1)} %maximum_bitcast_fusion.refs_0_), channel_id=1, source_target_pairs={{0,4},{2,6},{4,0},{6,2},{8,12},{10,14},{12,8},{14,10},{1,5},{3,7},... | collective-permute-start | bytes 393224 | tf_op jit(solution)/shard_map/ppermute | solution.py:253
  4.2 10.5 %collective-permute-start.3 = (bf16[2,2,128,128]{3,2,1,0:T(8,128)(2,1)S(1)}, bf16[2,2,128,128]{3,2,1,0:T(8,128)(2,1)S(1)}, u32[]{:S(2)}, u32[]{:S(2)}) collective-permute-start(bf16[2,2,128,128]{3,2,1,0:T(8,128)(2,1)S(1)} %maximum_bitcast_fusion.refs_0_), channel_id=1, source_target_pairs={{0,2},{2,0},{4,6},{6,4},{8,10},{10,8},{12,14},{14,12},{1,3},{3,1},... | collective-permute-start | bytes 393224 | tf_op jit(solution)/shard_map/ppermute | solution.py:253
  9.2 7.9 %collective-permute-start.4 = (bf16[2,2,128,128]{3,2,1,0:T(8,128)(2,1)S(1)}, bf16[2,2,128,128]{3,2,1,0:T(8,128)(2,1)S(1)}, u32[]{:S(2)}, u32[]{:S(2)}) collective-permute-start(bf16[2,2,128,128]{3,2,1,0:T(8,128)(2,1)S(1)} %collective-permute-done.refs_4_), channel_id=1, source_target_pairs={{8,14},{10,12},{12,10},{14,8},{9,15},{11,13},{13,11},{15,9},{24,30... | collective-permute-start | bytes 393224 | tf_op jit(solution)/shard_map/ppermute | solution.py:253
  12.1 6.5 %collective-permute-start.5 = (bf16[2,2,128,128]{3,2,1,0:T(8,128)(2,1)S(1)}, bf16[2,2,128,128]{3,2,1,0:T(8,128)(2,1)S(1)}, u32[]{:S(2)}, u32[]{:S(2)}) collective-permute-start(bf16[2,2,128,128]{3,2,1,0:T(8,128)(2,1)S(1)} %collective-permute-done.refs_4_), channel_id=1, source_target_pairs={{0,4},{2,6},{4,0},{6,2},{8,12},{10,14},{12,8},{14,10},{1,5},{3,7},... | collective-permute-start | bytes 393224 | tf_op jit(solution)/shard_map/ppermute | solution.py:253
  14.1 5.0 %collective-permute-start.6 = (bf16[2,2,128,128]{3,2,1,0:T(8,128)(2,1)S(1)}, bf16[2,2,128,128]{3,2,1,0:T(8,128)(2,1)S(1)}, u32[]{:S(2)}, u32[]{:S(2)}) collective-permute-start(bf16[2,2,128,128]{3,2,1,0:T(8,128)(2,1)S(1)} %collective-permute-done.refs_4_), channel_id=1, source_target_pairs={{0,2},{2,0},{4,6},{6,4},{8,10},{10,8},{12,14},{14,12},{1,3},{3,1},... | collective-permute-start | bytes 393224 | tf_op jit(solution)/shard_map/ppermute | solution.py:253

commit v4 on v3

--- a/solution.py
+++ b/solution.py
@@ -11,8 +11,6 @@
 MASKED = -1e30
 ROW_TILE = 256
 HEADROOM = 60.0
-NEAR = (3, 2, 1)
-SPREAD = (3, 2, 1)
 
 
 def key_bias(lengths, own, block, rows):
@@ -248,15 +246,22 @@
     )(lhs, bias, *state, *pieces)
 
 
-def attend_exchanged(queries, block, lengths):
-    def swap(array, code, members=range(8)):
-        return lax.ppermute(array, "ctx", [(i, i ^ code) for i in members])
+def attend_exchanged(groups, queries, block, lengths):
+    def swap(array, code, lower_code=None, flip=0):
+        lower_code = code if lower_code is None else lower_code
+        pairs = []
+        for g in range(groups):
+            for i in range(8):
+                target = (g, i ^ code) if i >= 4 else (g ^ flip, i ^ lower_code)
+                pairs.append((g * 8 + i, target[0] * 8 + target[1]))
+        return lax.ppermute(array, ("groups", "ctx"), pairs)
 
     crossed = swap(block, 6)
-    near = [swap(block, code) for code in NEAR]
-    lhs, bias = make_ready(queries, (0, *NEAR, 6, *[6 ^ code for code in SPREAD]), lengths)
+    near = [swap(block, code) for code in (3, 2, 1)]
+    lhs, bias = make_ready(queries, (0, 3, 2, 1, 6, 5, 4, 7), lengths)
     crossed, lhs = lax.optimization_barrier((crossed, lhs))
-    spread = [swap(crossed, code, range(4, 8) if code == 3 else range(8)) for code in SPREAD]
+    aside = dict(lower_code=0, flip=1) if groups % 2 == 0 else dict(lower_code=1)
+    spread = [swap(crossed, 3, **aside), swap(crossed, 2), swap(crossed, 1)]
     state = attend_near(queries.shape, lhs, bias, [block, *near, crossed])
     state = attend_middle(lhs, bias, 5, state, spread[:1])
     return attend_far(lhs, bias, 6, state, spread[1:])
@@ -333,11 +338,11 @@
     )(lengths, queries, blocks)
 
 
-def on_device(ctx, queries, keys, values, seq_lengths):
+def on_device(groups, ctx, queries, keys, values, seq_lengths):
     block = jnp.stack([keys, values]).transpose(0, 2, 1, 3)
     if ctx != 8:
         return attend_gathered(queries, lax.all_gather(block, "ctx"), seq_lengths)
-    return attend_exchanged(queries, block, seq_lengths)
+    return attend_exchanged(groups, queries, block, seq_lengths)
 
 
 def solution(mesh):
@@ -348,7 +353,7 @@
         P("groups"),
     )
     return jax.shard_map(
-        functools.partial(on_device, mesh.shape["ctx"]),
+        functools.partial(on_device, mesh.shape["groups"], mesh.shape["ctx"]),
         mesh=mesh,
         in_specs=placed,
         out_specs=P(("groups", "ctx"), "kvh", None, None),

time: 21.1 us -> 20.5 us (0.972)
  starting transfers between devices: 9.08 us -> 7.11 us
  waiting for transfers between devices: 4.62 us -> 6.03 us
    ppermute x7, starting transfers between devices: 9.08 us -> 7.11 us  [swap(): return lax.ppermute(array, ('groups', 'ctx'), pairs)]
    ppermute x7, waiting for transfers between devices: 4.62 us -> 6.03 us  [swap(): return lax.ppermute(array, ('groups', 'ctx'), pairs)]
  transfers between devices with their start and end apart: 7 -> 7, of which waited for: 4 -> 4; matrix products, arithmetic and copies ran while one was open for 0% -> 0% of each run, Pallas kernels for 21% -> 22%
where the time goes in v4:
time: 20.5 us; the launch traced here: 20.3 us
  starting transfers between devices  7.11 us (35%)
  Pallas kernels  6.21 us (30%)
  waiting for transfers between devices  6.03 us (29%)
  local copies, waits for them, and re-layouts  0.89 us (4%)
    ppermute x7, starting transfers between devices, swap(): return lax.ppermute(array, ('groups', 'ctx'), pairs)  7.11 us
    ppermute x7, waiting for transfers between devices, swap(): return lax.ppermute(array, ('groups', 'ctx'), pairs)  6.03 us
    pallas_call x1, Pallas kernels, attend_near(): pl.pallas_call(near_kernel, out_shape=(jax.ShapeDtypeStruct(shape, jnp.bf...  2.3 us
    pallas_call x1, Pallas kernels, attend_far(): pl.pallas_call(functools.partial(far_kernel, skip), out_shape=jax.ShapeDt...  1.81 us
    pallas_call x1, Pallas kernels, make_ready(): pl.pallas_call(functools.partial(ready_kernel, codes), out_shape=(jax.Sha...  1.15 us
    pallas_call x1, Pallas kernels, attend_middle(): pl.pallas_call(functools.partial(middle_kernel, skip), out_shape=(jax.Sha...  0.96 us
    another operation x1, local copies, waits for them, and re-layouts, on_device(): block = jnp.stack([keys, values]).transpose(0, 2, 1, 3)  0.89 us
  transfers between devices with their start and end apart: 7, of which 4 were waited for; matrix products, arithmetic and copies ran while one was open for 0% of the time, Pallas kernels for 22%

profile of v4, /device:TPU:24, one launch (start us, length us, event | category | flops | bytes accessed | tf_op | source)
XLA Modules:
  0.0 20.3 jit_solution(12735407209312708559)
XLA Ops:
  0.0 0.9 %copy_bitcast_fusion = (bf16[1,128,2,128]{3,1,2,0:T(8,128)(2,1)S(1)}, bf16[1,128,2,128]{3,1,2,0:T(8,128)(2,1)S(1)}) fusion(bf16[128,2,128]{2,1,0:T(2,128)(2,1)} %param.6, bf16[128,2,128]{2,1,0:T(2,128)(2,1)} %param.5), kind=kLoop, calls=%fused_computation.1 | loop fusion | bytes 262144 | tf_op jit(solution)/shard_map/stack | solution.py:342
  0.9 0.1 collective-permute-start
  1.0 1.8 %collective-permute-start.1 = (bf16[2,2,128,128]{3,2,1,0:T(8,128)(2,1)S(1)}, bf16[2,2,128,128]{3,2,1,0:T(8,128)(2,1)S(1)}, u32[]{:S(2)}, u32[]{:S(2)}) collective-permute-start(bf16[2,2,128,128]{3,2,1,0:T(8,128)(2,1)S(1)} %maximum_bitcast_fusion.refs_0_), channel_id=1, source_target_pairs={{0,6},{2,4},{4,2},{6,0},{8,14},{10,12},{12,10},{14,8},{16,22},{18,... | collective-permute-start | bytes 393224 | tf_op jit(solution)/shard_map/ppermute | solution.py:257
  2.8 1.3 %collective-permute-start.2 = (bf16[2,2,128,128]{3,2,1,0:T(8,128)(2,1)S(1)}, bf16[2,2,128,128]{3,2,1,0:T(8,128)(2,1)S(1)}, u32[]{:S(2)}, u32[]{:S(2)}) collective-permute-start(bf16[2,2,128,128]{3,2,1,0:T(8,128)(2,1)S(1)} %maximum_bitcast_fusion.refs_0_), channel_id=1, source_target_pairs={{0,4},{2,6},{4,0},{6,2},{8,12},{10,14},{12,8},{14,10},{16,20},{18,... | collective-permute-start | bytes 393224 | tf_op jit(solution)/shard_map/ppermute | solution.py:257
  4.2 0.4 %collective-permute-start.3 = (bf16[2,2,128,128]{3,2,1,0:T(8,128)(2,1)S(1)}, bf16[2,2,128,128]{3,2,1,0:T(8,128)(2,1)S(1)}, u32[]{:S(2)}, u32[]{:S(2)}) collective-permute-start(bf16[2,2,128,128]{3,2,1,0:T(8,128)(2,1)S(1)} %maximum_bitcast_fusion.refs_0_), channel_id=1, source_target_pairs={{0,2},{2,0},{4,6},{6,4},{8,10},{10,8},{12,14},{14,12},{16,18},{18,... | collective-permute-start | bytes 393224 | tf_op jit(solution)/shard_map/ppermute | solution.py:257
  4.6 1.1 %ready.1 = (bf16[2,1024,256]{2,1,0:T(8,128)(2,1)S(1)}, bf16[8,128,128]{2,1,0:T(8,128)(2,1)S(1)}) custom-call(s32[4]{0:T(128)} %lengths_hbm.1, bf16[128,2,8,128]{3,2,1,0:T(8,128)(2,1)} %query_hbm.1), custom_call_target="tpu_custom_call" | custom-call | tf_op jit(solution)/shard_map/ready/pallas_call | solution.py:183
  5.7 3.5 %collective-permute-done.refs_4_ = bf16[2,2,128,128]{3,2,1,0:T(8,128)(2,1)S(1)} collective-permute-done((bf16[2,2,128,128]{3,2,1,0:T(8,128)(2,1)S(1)}, bf16[2,2,128,128]{3,2,1,0:T(8,128)(2,1)S(1)}, u32[]{:S(2)}, u32[]{:S(2)}) %collective-permute-start) | collective-permute-done | bytes 131104 | tf_op jit(solution)/shard_map/ppermute | solution.py:257
  9.2 1.0 %collective-permute-start.4 = (bf16[2,2,128,128]{3,2,1,0:T(8,128)(2,1)S(1)}, bf16[2,2,128,128]{3,2,1,0:T(8,128)(2,1)S(1)}, u32[]{:S(2)}, u32[]{:S(2)}) collective-permute-start(bf16[2,2,128,128]{3,2,1,0:T(8,128)(2,1)S(1)} %collective-permute-done.refs_4_), channel_id=1, source_target_pairs={{0,16},{2,18},{4,20},{6,22},{8,14},{10,12},{12,10},{14,8},{16,0},{... | collective-permute-start | bytes 393224 | tf_op jit(solution)/shard_map/ppermute | solution.py:257
  10.1 2.0 %collective-permute-start.5 = (bf16[2,2,128,128]{3,2,1,0:T(8,128)(2,1)S(1)}, bf16[2,2,128,128]{3,2,1,0:T(8,128)(2,1)S(1)}, u32[]{:S(2)}, u32[]{:S(2)}) collective-permute-start(bf16[2,2,128,128]{3,2,1,0:T(8,128)(2,1)S(1)} %collective-permute-done.refs_4_), channel_id=1, source_target_pairs={{0,4},{2,6},{4,0},{6,2},{8,12},{10,14},{12,8},{14,10},{16,20},{18,... | collective-permute-start | bytes 393224 | tf_op jit(solution)/shard_map/ppermute | solution.py:257
  12.1 0.0 collective-permute-done.1.refs_1_
  12.1 0.5 %collective-permute-start.6 = (bf16[2,2,128,128]{3,2,1,0:T(8,128)(2,1)S(1)}, bf16[2,2,128,128]{3,2,1,0:T(8,128)(2,1)S(1)}, u32[]{:S(2)}, u32[]{:S(2)}) collective-permute-start(bf16[2,2,128,128]{3,2,1,0:T(8,128)(2,1)S(1)} %collective-permute-done.refs_4_), channel_id=1, source_target_pairs={{0,2},{2,0},{4,6},{6,4},{8,10},{10,8},{12,14},{14,12},{16,18},{18,... | collective-permute-start | bytes 393224 | tf_op jit(solution)/shard_map/ppermute | solution.py:257
  12.7 1.1 %collective-permute-done.2.refs_2_ = bf16[2,2,128,128]{3,2,1,0:T(8,128)(2,1)S(1)} collective-permute-done((bf16[2,2,128,128]{3,2,1,0:T(8,128)(2,1)S(1)}, bf16[2,2,128,128]{3,2,1,0:T(8,128)(2,1)S(1)}, u32[]{:S(2)}, u32[]{:S(2)}) %collective-permute-start.2) | collective-permute-done | bytes 131104 | tf_op jit(solution)/shard_map/ppermute | solution.py:257
  13.8 0.0 collective-permute-done.3.refs_3_
  13.8 2.3 %near.1 = (bf16[128,2,8,128]{3,2,1,0:T(8,128)(2,1)}, f32[2,1024,128]{2,1,0:T(8,128)S(1)}, f32[2,1024,256]{2,1,0:T(8,128)S(1)}) custom-call(bf16[2,1024,256]{2,1,0:T(8,128)(2,1)S(1)} %get-tuple-element.15.lhs_ref, bf16[8,128,128]{2,1,0:T(8,128)(2,1)S(1)} %get-tuple-element.16.bias_ref, bf16[2,2,128,128]{3,2,1,0:T(8,128)(2,1)S(1)} %maximum_bitcast_fusion.refs_0_, ...), custom_call_target="tpu_custom_call" | custom-call | tf_op jit(solution)/shard_map/near/pallas_call | solution.py:207
  16.1 0.7 %collective-permute-done.4.refs_0_ = bf16[2,2,128,128]{3,2,1,0:T(8,128)(2,1)S(1)} collective-permute-done((bf16[2,2,128,128]{3,2,1,0:T(8,128)(2,1)S(1)}, bf16[2,2,128,128]{3,2,1,0:T(8,128)(2,1)S(1)}, u32[]{:S(2)}, u32[]{:S(2)}) %collective-permute-start.4) | collective-permute-done | bytes 131104 | tf_op jit(solution)/shard_map/ppermute | solution.py:257
  16.8 1.0 %middle.1 = (f32[2,1024,128]{2,1,0:T(8,128)S(1)}, f32[2,1024,256]{2,1,0:T(8,128)S(1)}) custom-call(bf16[2,1024,256]{2,1,0:T(8,128)(2,1)S(1)} %get-tuple-element.15.lhs_ref, bf16[8,128,128]{2,1,0:T(8,128)(2,1)S(1)} %get-tuple-element.16.bias_ref, f32[2,1024,128]{2,1,0:T(8,128)S(1)} %get-tuple-element.19.peak_ref, ...), custom_call_target="tpu_custom_call" | custom-call | tf_op jit(solution)/shard_map/middle/pallas_call | solution.py:224
  17.7 0.8 %collective-permute-done.5.refs_0_ = bf16[2,2,128,128]{3,2,1,0:T(8,128)(2,1)S(1)} collective-permute-done((bf16[2,2,128,128]{3,2,1,0:T(8,128)(2,1)S(1)}, bf16[2,2,128,128]{3,2,1,0:T(8,128)(2,1)S(1)}, u32[]{:S(2)}, u32[]{:S(2)}) %collective-permute-start.5) | collective-permute-done | bytes 131104 | tf_op jit(solution)/shard_map/ppermute | solution.py:257
  18.5 0.0 collective-permute-done.6.refs_1_
  18.5 1.8 %far.1 = bf16[128,2,8,128]{3,2,1,0:T(8,128)(2,1)} custom-call(bf16[2,1024,256]{2,1,0:T(8,128)(2,1)S(1)} %get-tuple-element.15.lhs_ref, bf16[8,128,128]{2,1,0:T(8,128)(2,1)S(1)} %get-tuple-element.16.bias_ref, bf16[128,2,8,128]{3,2,1,0:T(8,128)(2,1)} %get-tuple-element.18._, ...), custom_call_target="tpu_custom_call", output_to_operand_aliasing={{}: (2, {})} | custom-call | tf_op jit(solution)/shard_map/far/pallas_call | solution.py:237
  (1 shorter events, 0.0 us)
Async XLA Ops:
  0.9 8.3 %collective-permute-start = (bf16[2,2,128,128]{3,2,1,0:T(8,128)(2,1)S(1)}, bf16[2,2,128,128]{3,2,1,0:T(8,128)(2,1)S(1)}, u32[]{:S(2)}, u32[]{:S(2)}) collective-permute-start(bf16[2,2,128,128]{3,2,1,0:T(8,128)(2,1)S(1)} %maximum_bitcast_fusion.refs_0_), channel_id=1, source_target_pairs={{0,12},{2,14},{4,8},{6,10},{8,4},{10,6},{12,0},{14,2},{16,28},{18,... | collective-permute-start | bytes 393224 | tf_op jit(solution)/shard_map/ppermute | solution.py:257
  1.0 11.1 %collective-permute-start.1 = (bf16[2,2,128,128]{3,2,1,0:T(8,128)(2,1)S(1)}, bf16[2,2,128,128]{3,2,1,0:T(8,128)(2,1)S(1)}, u32[]{:S(2)}, u32[]{:S(2)}) collective-permute-start(bf16[2,2,128,128]{3,2,1,0:T(8,128)(2,1)S(1)} %maximum_bitcast_fusion.refs_0_), channel_id=1, source_target_pairs={{0,6},{2,4},{4,2},{6,0},{8,14},{10,12},{12,10},{14,8},{16,22},{18,... | collective-permute-start | bytes 393224 | tf_op jit(solution)/shard_map/ppermute | solution.py:257
  2.8 11.0 %collective-permute-start.2 = (bf16[2,2,128,128]{3,2,1,0:T(8,128)(2,1)S(1)}, bf16[2,2,128,128]{3,2,1,0:T(8,128)(2,1)S(1)}, u32[]{:S(2)}, u32[]{:S(2)}) collective-permute-start(bf16[2,2,128,128]{3,2,1,0:T(8,128)(2,1)S(1)} %maximum_bitcast_fusion.refs_0_), channel_id=1, source_target_pairs={{0,4},{2,6},{4,0},{6,2},{8,12},{10,14},{12,8},{14,10},{16,20},{18,... | collective-permute-start | bytes 393224 | tf_op jit(solution)/shard_map/ppermute | solution.py:257
  4.2 9.6 %collective-permute-start.3 = (bf16[2,2,128,128]{3,2,1,0:T(8,128)(2,1)S(1)}, bf16[2,2,128,128]{3,2,1,0:T(8,128)(2,1)S(1)}, u32[]{:S(2)}, u32[]{:S(2)}) collective-permute-start(bf16[2,2,128,128]{3,2,1,0:T(8,128)(2,1)S(1)} %maximum_bitcast_fusion.refs_0_), channel_id=1, source_target_pairs={{0,2},{2,0},{4,6},{6,4},{8,10},{10,8},{12,14},{14,12},{16,18},{18,... | collective-permute-start | bytes 393224 | tf_op jit(solution)/shard_map/ppermute | solution.py:257
  9.2 7.6 %collective-permute-start.4 = (bf16[2,2,128,128]{3,2,1,0:T(8,128)(2,1)S(1)}, bf16[2,2,128,128]{3,2,1,0:T(8,128)(2,1)S(1)}, u32[]{:S(2)}, u32[]{:S(2)}) collective-permute-start(bf16[2,2,128,128]{3,2,1,0:T(8,128)(2,1)S(1)} %collective-permute-done.refs_4_), channel_id=1, source_target_pairs={{0,16},{2,18},{4,20},{6,22},{8,14},{10,12},{12,10},{14,8},{16,0},{... | collective-permute-start | bytes 393224 | tf_op jit(solution)/shard_map/ppermute | solution.py:257
  10.1 8.3 %collective-permute-start.5 = (bf16[2,2,128,128]{3,2,1,0:T(8,128)(2,1)S(1)}, bf16[2,2,128,128]{3,2,1,0:T(8,128)(2,1)S(1)}, u32[]{:S(2)}, u32[]{:S(2)}) collective-permute-start(bf16[2,2,128,128]{3,2,1,0:T(8,128)(2,1)S(1)} %collective-permute-done.refs_4_), channel_id=1, source_target_pairs={{0,4},{2,6},{4,0},{6,2},{8,12},{10,14},{12,8},{14,10},{16,20},{18,... | collective-permute-start | bytes 393224 | tf_op jit(solution)/shard_map/ppermute | solution.py:257
  12.1 6.4 %collective-permute-start.6 = (bf16[2,2,128,128]{3,2,1,0:T(8,128)(2,1)S(1)}, bf16[2,2,128,128]{3,2,1,0:T(8,128)(2,1)S(1)}, u32[]{:S(2)}, u32[]{:S(2)}) collective-permute-start(bf16[2,2,128,128]{3,2,1,0:T(8,128)(2,1)S(1)} %collective-permute-done.refs_4_), channel_id=1, source_target_pairs={{0,2},{2,0},{4,6},{6,4},{8,10},{10,8},{12,14},{14,12},{16,18},{18,... | collective-permute-start | bytes 393224 | tf_op jit(solution)/shard_map/ppermute | solution.py:257

commit v5 on v4

--- a/solution.py
+++ b/solution.py
@@ -256,12 +256,13 @@
                 pairs.append((g * 8 + i, target[0] * 8 + target[1]))
         return lax.ppermute(array, ("groups", "ctx"), pairs)
 
+    diagonal = [(g * 8 + i, g * 8 + t) for g in range(groups) for i, t in enumerate((3, 2, 0, 1, 7, 6, 4, 5))]
     crossed = swap(block, 6)
-    near = [swap(block, code) for code in (3, 2, 1)]
-    lhs, bias = make_ready(queries, (0, 3, 2, 1, 6, 5, 4, 7), lengths)
+    near = [swap(block, 2), lax.ppermute(block, ("groups", "ctx"), diagonal), swap(block, 1)]
+    lhs, bias = make_ready(queries, (0, 2, 3, 1, 6, 5, 4, 7), lengths)
     crossed, lhs = lax.optimization_barrier((crossed, lhs))
     aside = dict(lower_code=0, flip=1) if groups % 2 == 0 else dict(lower_code=1)
-    spread = [swap(crossed, 3, **aside), swap(crossed, 2), swap(crossed, 1)]
+    spread = [swap(crossed, 3, **aside), swap(crossed, 2, **aside), swap(crossed, 1)]
     state = attend_near(queries.shape, lhs, bias, [block, *near, crossed])
     state = attend_middle(lhs, bias, 5, state, spread[:1])
     return attend_far(lhs, bias, 6, state, spread[1:])

time: 20.5 us -> 20.4 us (level)
  waiting for transfers between devices: 6.03 us -> 5.81 us
    ppermute x7 -> x6, waiting for transfers between devices: 6.03 us -> 4.21 us  [swap(): return lax.ppermute(array, ('groups', 'ctx'), pairs)]
    ppermute x0 -> x1, waiting for transfers between devices: none -> 1.6 us  [attend_exchanged(): lax.ppermute(block, ('groups', 'ctx'), diagonal)]
    ppermute x0 -> x1, starting transfers between devices: none -> 1.21 us  [attend_exchanged(): lax.ppermute(block, ('groups', 'ctx'), diagonal)]
    ppermute x7 -> x6, starting transfers between devices: 7.11 us -> 6.08 us  [swap(): return lax.ppermute(array, ('groups', 'ctx'), pairs)]
where the time goes in v5:
time: 20.4 us; the launch traced here: 20.3 us
  starting transfers between devices  7.29 us (36%)
  Pallas kernels  6.21 us (30%)
  waiting for transfers between devices  5.81 us (28%)
  local copies, waits for them, and re-layouts  0.89 us (4%)
    ppermute x6, starting transfers between devices, swap(): return lax.ppermute(array, ('groups', 'ctx'), pairs)  6.08 us
    ppermute x6, waiting for transfers between devices, swap(): return lax.ppermute(array, ('groups', 'ctx'), pairs)  4.21 us
    pallas_call x1, Pallas kernels, attend_near(): pl.pallas_call(near_kernel, out_shape=(jax.ShapeDtypeStruct(shape, jnp.bf...  2.3 us
    pallas_call x1, Pallas kernels, attend_far(): pl.pallas_call(functools.partial(far_kernel, skip), out_shape=jax.ShapeDt...  1.81 us
    ppermute x1, waiting for transfers between devices, attend_exchanged(): lax.ppermute(block, ('groups', 'ctx'), diagonal)  1.6 us
    ppermute x1, starting transfers between devices, attend_exchanged(): lax.ppermute(block, ('groups', 'ctx'), diagonal)  1.21 us
    pallas_call x1, Pallas kernels, make_ready(): pl.pallas_call(functools.partial(ready_kernel, codes), out_shape=(jax.Sha...  1.15 us
    pallas_call x1, Pallas kernels, attend_middle(): pl.pallas_call(functools.partial(middle_kernel, skip), out_shape=(jax.Sha...  0.96 us
  transfers between devices with their start and end apart: 7, of which 4 were waited for; matrix products, arithmetic and copies ran while one was open for 0% of the time, Pallas kernels for 22%

profile of v5, /device:TPU:24, one launch (start us, length us, event | category | flops | bytes accessed | tf_op | source)
XLA Modules:
  0.0 20.3 jit_solution(7558836617707793296)
XLA Ops:
  0.0 0.9 %copy_bitcast_fusion = (bf16[1,128,2,128]{3,1,2,0:T(8,128)(2,1)S(1)}, bf16[1,128,2,128]{3,1,2,0:T(8,128)(2,1)S(1)}) fusion(bf16[128,2,128]{2,1,0:T(2,128)(2,1)} %param.6, bf16[128,2,128]{2,1,0:T(2,128)(2,1)} %param.5), kind=kLoop, calls=%fused_computation.1 | loop fusion | bytes 262144 | tf_op jit(solution)/shard_map/stack | solution.py:343
  0.9 0.1 collective-permute-start
  1.0 0.9 %collective-permute-start.1 = (bf16[2,2,128,128]{3,2,1,0:T(8,128)(2,1)S(1)}, bf16[2,2,128,128]{3,2,1,0:T(8,128)(2,1)S(1)}, u32[]{:S(2)}, u32[]{:S(2)}) collective-permute-start(bf16[2,2,128,128]{3,2,1,0:T(8,128)(2,1)S(1)} %maximum_bitcast_fusion.refs_0_), channel_id=1, source_target_pairs={{0,4},{2,6},{4,0},{6,2},{8,12},{10,14},{12,8},{14,10},{16,20},{18,... | collective-permute-start | bytes 393224 | tf_op jit(solution)/shard_map/ppermute | solution.py:257
  1.9 1.2 %collective-permute-start.2 = (bf16[2,2,128,128]{3,2,1,0:T(8,128)(2,1)S(1)}, bf16[2,2,128,128]{3,2,1,0:T(8,128)(2,1)S(1)}, u32[]{:S(2)}, u32[]{:S(2)}) collective-permute-start(bf16[2,2,128,128]{3,2,1,0:T(8,128)(2,1)S(1)} %maximum_bitcast_fusion.refs_0_), channel_id=1, source_target_pairs={{0,6},{2,4},{4,0},{6,2},{8,14},{10,12},{12,8},{14,10},{16,22},{18,... | collective-permute-start | bytes 393224 | tf_op jit(solution)/shard_map/ppermute | solution.py:261
  3.1 1.6 %collective-permute-start.3 = (bf16[2,2,128,128]{3,2,1,0:T(8,128)(2,1)S(1)}, bf16[2,2,128,128]{3,2,1,0:T(8,128)(2,1)S(1)}, u32[]{:S(2)}, u32[]{:S(2)}) collective-permute-start(bf16[2,2,128,128]{3,2,1,0:T(8,128)(2,1)S(1)} %maximum_bitcast_fusion.refs_0_), channel_id=1, source_target_pairs={{0,2},{2,0},{4,6},{6,4},{8,10},{10,8},{12,14},{14,12},{16,18},{18,... | collective-permute-start | bytes 393224 | tf_op jit(solution)/shard_map/ppermute | solution.py:257
  4.7 1.1 %ready.1 = (bf16[2,1024,256]{2,1,0:T(8,128)(2,1)S(1)}, bf16[8,128,128]{2,1,0:T(8,128)(2,1)S(1)}) custom-call(s32[4]{0:T(128)} %lengths_hbm.1, bf16[128,2,8,128]{3,2,1,0:T(8,128)(2,1)} %query_hbm.1), custom_call_target="tpu_custom_call" | custom-call | tf_op jit(solution)/shard_map/ready/pallas_call | solution.py:183
  5.9 3.3 %collective-permute-done.refs_4_ = bf16[2,2,128,128]{3,2,1,0:T(8,128)(2,1)S(1)} collective-permute-done((bf16[2,2,128,128]{3,2,1,0:T(8,128)(2,1)S(1)}, bf16[2,2,128,128]{3,2,1,0:T(8,128)(2,1)S(1)}, u32[]{:S(2)}, u32[]{:S(2)}) %collective-permute-start) | collective-permute-done | bytes 131104 | tf_op jit(solution)/shard_map/ppermute | solution.py:257
  9.2 1.0 %collective-permute-start.4 = (bf16[2,2,128,128]{3,2,1,0:T(8,128)(2,1)S(1)}, bf16[2,2,128,128]{3,2,1,0:T(8,128)(2,1)S(1)}, u32[]{:S(2)}, u32[]{:S(2)}) collective-permute-start(bf16[2,2,128,128]{3,2,1,0:T(8,128)(2,1)S(1)} %collective-permute-done.refs_4_), channel_id=1, source_target_pairs={{0,16},{2,18},{4,20},{6,22},{8,14},{10,12},{12,10},{14,8},{16,0},{... | collective-permute-start | bytes 393224 | tf_op jit(solution)/shard_map/ppermute | solution.py:257
  10.1 2.0 %collective-permute-start.5 = (bf16[2,2,128,128]{3,2,1,0:T(8,128)(2,1)S(1)}, bf16[2,2,128,128]{3,2,1,0:T(8,128)(2,1)S(1)}, u32[]{:S(2)}, u32[]{:S(2)}) collective-permute-start(bf16[2,2,128,128]{3,2,1,0:T(8,128)(2,1)S(1)} %collective-permute-done.refs_4_), channel_id=1, source_target_pairs={{0,16},{2,18},{4,20},{6,22},{8,12},{10,14},{12,8},{14,10},{16,0},{... | collective-permute-start | bytes 393224 | tf_op jit(solution)/shard_map/ppermute | solution.py:257
  12.1 0.0 collective-permute-done.1.refs_1_
  12.1 0.5 %collective-permute-start.6 = (bf16[2,2,128,128]{3,2,1,0:T(8,128)(2,1)S(1)}, bf16[2,2,128,128]{3,2,1,0:T(8,128)(2,1)S(1)}, u32[]{:S(2)}, u32[]{:S(2)}) collective-permute-start(bf16[2,2,128,128]{3,2,1,0:T(8,128)(2,1)S(1)} %collective-permute-done.refs_4_), channel_id=1, source_target_pairs={{0,2},{2,0},{4,6},{6,4},{8,10},{10,8},{12,14},{14,12},{16,18},{18,... | collective-permute-start | bytes 393224 | tf_op jit(solution)/shard_map/ppermute | solution.py:257
  12.7 1.6 %collective-permute-done.2.refs_2_ = bf16[2,2,128,128]{3,2,1,0:T(8,128)(2,1)S(1)} collective-permute-done((bf16[2,2,128,128]{3,2,1,0:T(8,128)(2,1)S(1)}, bf16[2,2,128,128]{3,2,1,0:T(8,128)(2,1)S(1)}, u32[]{:S(2)}, u32[]{:S(2)}) %collective-permute-start.2) | collective-permute-done | bytes 131104 | tf_op jit(solution)/shard_map/ppermute | solution.py:261
  14.3 0.0 collective-permute-done.3.refs_3_
  14.3 2.3 %near.1 = (bf16[128,2,8,128]{3,2,1,0:T(8,128)(2,1)}, f32[2,1024,128]{2,1,0:T(8,128)S(1)}, f32[2,1024,256]{2,1,0:T(8,128)S(1)}) custom-call(bf16[2,1024,256]{2,1,0:T(8,128)(2,1)S(1)} %get-tuple-element.15.lhs_ref, bf16[8,128,128]{2,1,0:T(8,128)(2,1)S(1)} %get-tuple-element.16.bias_ref, bf16[2,2,128,128]{3,2,1,0:T(8,128)(2,1)S(1)} %maximum_bitcast_fusion.refs_0_, ...), custom_call_target="tpu_custom_call" | custom-call | tf_op jit(solution)/shard_map/near/pallas_call | solution.py:207
  16.6 0.4 %collective-permute-done.4.refs_0_ = bf16[2,2,128,128]{3,2,1,0:T(8,128)(2,1)S(1)} collective-permute-done((bf16[2,2,128,128]{3,2,1,0:T(8,128)(2,1)S(1)}, bf16[2,2,128,128]{3,2,1,0:T(8,128)(2,1)S(1)}, u32[]{:S(2)}, u32[]{:S(2)}) %collective-permute-start.4) | collective-permute-done | bytes 131104 | tf_op jit(solution)/shard_map/ppermute | solution.py:257
  17.0 1.0 %middle.1 = (f32[2,1024,128]{2,1,0:T(8,128)S(1)}, f32[2,1024,256]{2,1,0:T(8,128)S(1)}) custom-call(bf16[2,1024,256]{2,1,0:T(8,128)(2,1)S(1)} %get-tuple-element.15.lhs_ref, bf16[8,128,128]{2,1,0:T(8,128)(2,1)S(1)} %get-tuple-element.16.bias_ref, f32[2,1024,128]{2,1,0:T(8,128)S(1)} %get-tuple-element.19.peak_ref, ...), custom_call_target="tpu_custom_call" | custom-call | tf_op jit(solution)/shard_map/middle/pallas_call | solution.py:224
  18.0 0.0 collective-permute-done.5.refs_0_
  18.0 0.5 %collective-permute-done.6.refs_1_ = bf16[2,2,128,128]{3,2,1,0:T(8,128)(2,1)S(1)} collective-permute-done((bf16[2,2,128,128]{3,2,1,0:T(8,128)(2,1)S(1)}, bf16[2,2,128,128]{3,2,1,0:T(8,128)(2,1)S(1)}, u32[]{:S(2)}, u32[]{:S(2)}) %collective-permute-start.6) | collective-permute-done | bytes 131104 | tf_op jit(solution)/shard_map/ppermute | solution.py:257
  18.5 1.8 %far.1 = bf16[128,2,8,128]{3,2,1,0:T(8,128)(2,1)} custom-call(bf16[2,1024,256]{2,1,0:T(8,128)(2,1)S(1)} %get-tuple-element.15.lhs_ref, bf16[8,128,128]{2,1,0:T(8,128)(2,1)S(1)} %get-tuple-element.16.bias_ref, bf16[128,2,8,128]{3,2,1,0:T(8,128)(2,1)} %get-tuple-element.18._, ...), custom_call_target="tpu_custom_call", output_to_operand_aliasing={{}: (2, {})} | custom-call | tf_op jit(solution)/shard_map/far/pallas_call | solution.py:237
  (1 shorter events, 0.0 us)
Async XLA Ops:
  0.9 8.3 %collective-permute-start = (bf16[2,2,128,128]{3,2,1,0:T(8,128)(2,1)S(1)}, bf16[2,2,128,128]{3,2,1,0:T(8,128)(2,1)S(1)}, u32[]{:S(2)}, u32[]{:S(2)}) collective-permute-start(bf16[2,2,128,128]{3,2,1,0:T(8,128)(2,1)S(1)} %maximum_bitcast_fusion.refs_0_), channel_id=1, source_target_pairs={{0,12},{2,14},{4,8},{6,10},{8,4},{10,6},{12,0},{14,2},{16,28},{18,... | collective-permute-start | bytes 393224 | tf_op jit(solution)/shard_map/ppermute | solution.py:257
  1.0 11.1 %collective-permute-start.1 = (bf16[2,2,128,128]{3,2,1,0:T(8,128)(2,1)S(1)}, bf16[2,2,128,128]{3,2,1,0:T(8,128)(2,1)S(1)}, u32[]{:S(2)}, u32[]{:S(2)}) collective-permute-start(bf16[2,2,128,128]{3,2,1,0:T(8,128)(2,1)S(1)} %maximum_bitcast_fusion.refs_0_), channel_id=1, source_target_pairs={{0,4},{2,6},{4,0},{6,2},{8,12},{10,14},{12,8},{14,10},{16,20},{18,... | collective-permute-start | bytes 393224 | tf_op jit(solution)/shard_map/ppermute | solution.py:257
  1.9 12.4 %collective-permute-start.2 = (bf16[2,2,128,128]{3,2,1,0:T(8,128)(2,1)S(1)}, bf16[2,2,128,128]{3,2,1,0:T(8,128)(2,1)S(1)}, u32[]{:S(2)}, u32[]{:S(2)}) collective-permute-start(bf16[2,2,128,128]{3,2,1,0:T(8,128)(2,1)S(1)} %maximum_bitcast_fusion.refs_0_), channel_id=1, source_target_pairs={{0,6},{2,4},{4,0},{6,2},{8,14},{10,12},{12,8},{14,10},{16,22},{18,... | collective-permute-start | bytes 393224 | tf_op jit(solution)/shard_map/ppermute | solution.py:261
  3.1 11.2 %collective-permute-start.3 = (bf16[2,2,128,128]{3,2,1,0:T(8,128)(2,1)S(1)}, bf16[2,2,128,128]{3,2,1,0:T(8,128)(2,1)S(1)}, u32[]{:S(2)}, u32[]{:S(2)}) collective-permute-start(bf16[2,2,128,128]{3,2,1,0:T(8,128)(2,1)S(1)} %maximum_bitcast_fusion.refs_0_), channel_id=1, source_target_pairs={{0,2},{2,0},{4,6},{6,4},{8,10},{10,8},{12,14},{14,12},{16,18},{18,... | collective-permute-start | bytes 393224 | tf_op jit(solution)/shard_map/ppermute | solution.py:257
  9.2 7.8 %collective-permute-start.4 = (bf16[2,2,128,128]{3,2,1,0:T(8,128)(2,1)S(1)}, bf16[2,2,128,128]{3,2,1,0:T(8,128)(2,1)S(1)}, u32[]{:S(2)}, u32[]{:S(2)}) collective-permute-start(bf16[2,2,128,128]{3,2,1,0:T(8,128)(2,1)S(1)} %collective-permute-done.refs_4_), channel_id=1, source_target_pairs={{0,16},{2,18},{4,20},{6,22},{8,14},{10,12},{12,10},{14,8},{16,0},{... | collective-permute-start | bytes 393224 | tf_op jit(solution)/shard_map/ppermute | solution.py:257
  10.1 7.8 %collective-permute-start.5 = (bf16[2,2,128,128]{3,2,1,0:T(8,128)(2,1)S(1)}, bf16[2,2,128,128]{3,2,1,0:T(8,128)(2,1)S(1)}, u32[]{:S(2)}, u32[]{:S(2)}) collective-permute-start(bf16[2,2,128,128]{3,2,1,0:T(8,128)(2,1)S(1)} %collective-permute-done.refs_4_), channel_id=1, source_target_pairs={{0,16},{2,18},{4,20},{6,22},{8,12},{10,14},{12,8},{14,10},{16,0},{... | collective-permute-start | bytes 393224 | tf_op jit(solution)/shard_map/ppermute | solution.py:257
  12.1 6.3 %collective-permute-start.6 = (bf16[2,2,128,128]{3,2,1,0:T(8,128)(2,1)S(1)}, bf16[2,2,128,128]{3,2,1,0:T(8,128)(2,1)S(1)}, u32[]{:S(2)}, u32[]{:S(2)}) collective-permute-start(bf16[2,2,128,128]{3,2,1,0:T(8,128)(2,1)S(1)} %collective-permute-done.refs_4_), channel_id=1, source_target_pairs={{0,2},{2,0},{4,6},{6,4},{8,10},{10,8},{12,14},{14,12},{16,18},{18,... | collective-permute-start | bytes 393224 | tf_op jit(solution)/shard_map/ppermute | solution.py:257

commit v6 on v4

--- a/solution.py
+++ b/solution.py
@@ -258,13 +258,13 @@
 
     crossed = swap(block, 6)
     near = [swap(block, code) for code in (3, 2, 1)]
-    lhs, bias = make_ready(queries, (0, 3, 2, 1, 6, 5, 4, 7), lengths)
+    lhs, bias = make_ready(queries, (0, 3, 2, 1, 6, 7, 5, 4), lengths)
     crossed, lhs = lax.optimization_barrier((crossed, lhs))
     aside = dict(lower_code=0, flip=1) if groups % 2 == 0 else dict(lower_code=1)
     spread = [swap(crossed, 3, **aside), swap(crossed, 2), swap(crossed, 1)]
     state = attend_near(queries.shape, lhs, bias, [block, *near, crossed])
-    state = attend_middle(lhs, bias, 5, state, spread[:1])
-    return attend_far(lhs, bias, 6, state, spread[1:])
+    state = attend_middle(lhs, bias, 5, state, spread[2:])
+    return attend_far(lhs, bias, 6, state, spread[:2])
 
 
 def stream_kernel(step, lengths, query_ref, block_ref, out_ref, peak_ref, both_ref):

time: 20.5 us -> 20.4 us (level)
  starting transfers between devices: 7.11 us -> 6.64 us
  waiting for transfers between devices: 6.03 us -> 6.44 us
    ppermute x7, starting transfers between devices: 7.11 us -> 6.64 us  [swap(): return lax.ppermute(array, ('groups', 'ctx'), pairs)]
    ppermute x7, waiting for transfers between devices: 6.03 us -> 6.44 us  [swap(): return lax.ppermute(array, ('groups', 'ctx'), pairs)]
where the time goes in v6:
time: 20.4 us; the launch traced here: 20.3 us
  starting transfers between devices  6.64 us (33%)
  waiting for transfers between devices  6.44 us (32%)
  Pallas kernels  6.22 us (30%)
  local copies, waits for them, and re-layouts  0.89 us (4%)
    ppermute x7, starting transfers between devices, swap(): return lax.ppermute(array, ('groups', 'ctx'), pairs)  6.64 us
    ppermute x7, waiting for transfers between devices, swap(): return lax.ppermute(array, ('groups', 'ctx'), pairs)  6.44 us
    pallas_call x1, Pallas kernels, attend_near(): pl.pallas_call(near_kernel, out_shape=(jax.ShapeDtypeStruct(shape, jnp.bf...  2.3 us
    pallas_call x1, Pallas kernels, attend_far(): pl.pallas_call(functools.partial(far_kernel, skip), out_shape=jax.ShapeDt...  1.81 us
    pallas_call x1, Pallas kernels, make_ready(): pl.pallas_call(functools.partial(ready_kernel, codes), out_shape=(jax.Sha...  1.15 us
    pallas_call x1, Pallas kernels, attend_middle(): pl.pallas_call(functools.partial(middle_kernel, skip), out_shape=(jax.Sha...  0.97 us
    another operation x1, local copies, waits for them, and re-layouts, on_device(): block = jnp.stack([keys, values]).transpose(0, 2, 1, 3)  0.89 us
  transfers between devices with their start and end apart: 7, of which 4 were waited for; matrix products, arithmetic and copies ran while one was open for 0% of the time, Pallas kernels for 22%

profile of v6, /device:TPU:24, one launch (start us, length us, event | category | flops | bytes accessed | tf_op | source)
XLA Modules:
  0.0 20.3 jit_solution(15799806962186742071)
XLA Ops:
  0.0 0.9 %copy_bitcast_fusion = (bf16[1,128,2,128]{3,1,2,0:T(8,128)(2,1)S(1)}, bf16[1,128,2,128]{3,1,2,0:T(8,128)(2,1)S(1)}) fusion(bf16[128,2,128]{2,1,0:T(2,128)(2,1)} %param.6, bf16[128,2,128]{2,1,0:T(2,128)(2,1)} %param.5), kind=kLoop, calls=%fused_computation.1 | loop fusion | bytes 262144 | tf_op jit(solution)/shard_map/stack | solution.py:342
  0.9 0.1 collective-permute-start
  1.0 1.8 %collective-permute-start.1 = (bf16[2,2,128,128]{3,2,1,0:T(8,128)(2,1)S(1)}, bf16[2,2,128,128]{3,2,1,0:T(8,128)(2,1)S(1)}, u32[]{:S(2)}, u32[]{:S(2)}) collective-permute-start(bf16[2,2,128,128]{3,2,1,0:T(8,128)(2,1)S(1)} %maximum_bitcast_fusion.refs_0_), channel_id=1, source_target_pairs={{0,6},{2,4},{4,2},{6,0},{8,14},{10,12},{12,10},{14,8},{16,22},{18,... | collective-permute-start | bytes 393224 | tf_op jit(solution)/shard_map/ppermute | solution.py:257
  2.8 1.3 %collective-permute-start.2 = (bf16[2,2,128,128]{3,2,1,0:T(8,128)(2,1)S(1)}, bf16[2,2,128,128]{3,2,1,0:T(8,128)(2,1)S(1)}, u32[]{:S(2)}, u32[]{:S(2)}) collective-permute-start(bf16[2,2,128,128]{3,2,1,0:T(8,128)(2,1)S(1)} %maximum_bitcast_fusion.refs_0_), channel_id=1, source_target_pairs={{0,4},{2,6},{4,0},{6,2},{8,12},{10,14},{12,8},{14,10},{16,20},{18,... | collective-permute-start | bytes 393224 | tf_op jit(solution)/shard_map/ppermute | solution.py:257
  4.2 0.4 %collective-permute-start.3 = (bf16[2,2,128,128]{3,2,1,0:T(8,128)(2,1)S(1)}, bf16[2,2,128,128]{3,2,1,0:T(8,128)(2,1)S(1)}, u32[]{:S(2)}, u32[]{:S(2)}) collective-permute-start(bf16[2,2,128,128]{3,2,1,0:T(8,128)(2,1)S(1)} %maximum_bitcast_fusion.refs_0_), channel_id=1, source_target_pairs={{0,2},{2,0},{4,6},{6,4},{8,10},{10,8},{12,14},{14,12},{16,18},{18,... | collective-permute-start | bytes 393224 | tf_op jit(solution)/shard_map/ppermute | solution.py:257
  4.6 1.1 %ready.1 = (bf16[2,1024,256]{2,1,0:T(8,128)(2,1)S(1)}, bf16[8,128,128]{2,1,0:T(8,128)(2,1)S(1)}) custom-call(s32[4]{0:T(128)} %lengths_hbm.1, bf16[128,2,8,128]{3,2,1,0:T(8,128)(2,1)} %query_hbm.1), custom_call_target="tpu_custom_call" | custom-call | tf_op jit(solution)/shard_map/ready/pallas_call | solution.py:183
  5.7 3.5 %collective-permute-done.refs_4_ = bf16[2,2,128,128]{3,2,1,0:T(8,128)(2,1)S(1)} collective-permute-done((bf16[2,2,128,128]{3,2,1,0:T(8,128)(2,1)S(1)}, bf16[2,2,128,128]{3,2,1,0:T(8,128)(2,1)S(1)}, u32[]{:S(2)}, u32[]{:S(2)}) %collective-permute-start) | collective-permute-done | bytes 131104 | tf_op jit(solution)/shard_map/ppermute | solution.py:257
  9.2 1.5 %collective-permute-start.4 = (bf16[2,2,128,128]{3,2,1,0:T(8,128)(2,1)S(1)}, bf16[2,2,128,128]{3,2,1,0:T(8,128)(2,1)S(1)}, u32[]{:S(2)}, u32[]{:S(2)}) collective-permute-start(bf16[2,2,128,128]{3,2,1,0:T(8,128)(2,1)S(1)} %collective-permute-done.refs_4_), channel_id=1, source_target_pairs={{0,2},{2,0},{4,6},{6,4},{8,10},{10,8},{12,14},{14,12},{16,18},{18,... | collective-permute-start | bytes 393224 | tf_op jit(solution)/shard_map/ppermute | solution.py:257
  10.7 0.0 collective-permute-start.5
  10.7 0.5 %collective-permute-done.1.refs_1_ = bf16[2,2,128,128]{3,2,1,0:T(8,128)(2,1)S(1)} collective-permute-done((bf16[2,2,128,128]{3,2,1,0:T(8,128)(2,1)S(1)}, bf16[2,2,128,128]{3,2,1,0:T(8,128)(2,1)S(1)}, u32[]{:S(2)}, u32[]{:S(2)}) %collective-permute-start.1) | collective-permute-done | bytes 131104 | tf_op jit(solution)/shard_map/ppermute | solution.py:257
  11.2 1.5 %collective-permute-start.6 = (bf16[2,2,128,128]{3,2,1,0:T(8,128)(2,1)S(1)}, bf16[2,2,128,128]{3,2,1,0:T(8,128)(2,1)S(1)}, u32[]{:S(2)}, u32[]{:S(2)}) collective-permute-start(bf16[2,2,128,128]{3,2,1,0:T(8,128)(2,1)S(1)} %collective-permute-done.refs_4_), channel_id=1, source_target_pairs={{0,4},{2,6},{4,0},{6,2},{8,12},{10,14},{12,8},{14,10},{16,20},{18,... | collective-permute-start | bytes 393224 | tf_op jit(solution)/shard_map/ppermute | solution.py:257
  12.7 1.1 %collective-permute-done.2.refs_2_ = bf16[2,2,128,128]{3,2,1,0:T(8,128)(2,1)S(1)} collective-permute-done((bf16[2,2,128,128]{3,2,1,0:T(8,128)(2,1)S(1)}, bf16[2,2,128,128]{3,2,1,0:T(8,128)(2,1)S(1)}, u32[]{:S(2)}, u32[]{:S(2)}) %collective-permute-start.2) | collective-permute-done | bytes 131104 | tf_op jit(solution)/shard_map/ppermute | solution.py:257
  13.8 0.0 collective-permute-done.3.refs_3_
  13.8 2.3 %near.1 = (bf16[128,2,8,128]{3,2,1,0:T(8,128)(2,1)}, f32[2,1024,128]{2,1,0:T(8,128)S(1)}, f32[2,1024,256]{2,1,0:T(8,128)S(1)}) custom-call(bf16[2,1024,256]{2,1,0:T(8,128)(2,1)S(1)} %get-tuple-element.15.lhs_ref, bf16[8,128,128]{2,1,0:T(8,128)(2,1)S(1)} %get-tuple-element.16.bias_ref, bf16[2,2,128,128]{3,2,1,0:T(8,128)(2,1)S(1)} %maximum_bitcast_fusion.refs_0_, ...), custom_call_target="tpu_custom_call" | custom-call | tf_op jit(solution)/shard_map/near/pallas_call | solution.py:207
  16.1 0.0 collective-permute-done.4.refs_0_
  16.1 1.0 %middle.1 = (f32[2,1024,128]{2,1,0:T(8,128)S(1)}, f32[2,1024,256]{2,1,0:T(8,128)S(1)}) custom-call(bf16[2,1024,256]{2,1,0:T(8,128)(2,1)S(1)} %get-tuple-element.15.lhs_ref, bf16[8,128,128]{2,1,0:T(8,128)(2,1)S(1)} %get-tuple-element.16.bias_ref, f32[2,1024,128]{2,1,0:T(8,128)S(1)} %get-tuple-element.19.peak_ref, ...), custom_call_target="tpu_custom_call" | custom-call | tf_op jit(solution)/shard_map/middle/pallas_call | solution.py:224
  17.1 0.0 collective-permute-done.5.refs_0_
  17.1 1.4 %collective-permute-done.6.refs_1_ = bf16[2,2,128,128]{3,2,1,0:T(8,128)(2,1)S(1)} collective-permute-done((bf16[2,2,128,128]{3,2,1,0:T(8,128)(2,1)S(1)}, bf16[2,2,128,128]{3,2,1,0:T(8,128)(2,1)S(1)}, u32[]{:S(2)}, u32[]{:S(2)}) %collective-permute-start.6) | collective-permute-done | bytes 131104 | tf_op jit(solution)/shard_map/ppermute | solution.py:257
  18.5 1.8 %far.1 = bf16[128,2,8,128]{3,2,1,0:T(8,128)(2,1)} custom-call(bf16[2,1024,256]{2,1,0:T(8,128)(2,1)S(1)} %get-tuple-element.15.lhs_ref, bf16[8,128,128]{2,1,0:T(8,128)(2,1)S(1)} %get-tuple-element.16.bias_ref, bf16[128,2,8,128]{3,2,1,0:T(8,128)(2,1)} %get-tuple-element.18._, ...), custom_call_target="tpu_custom_call", output_to_operand_aliasing={{}: (2, {})} | custom-call | tf_op jit(solution)/shard_map/far/pallas_call | solution.py:237
  (1 shorter events, 0.0 us)
Async XLA Ops:
  0.9 8.3 %collective-permute-start = (bf16[2,2,128,128]{3,2,1,0:T(8,128)(2,1)S(1)}, bf16[2,2,128,128]{3,2,1,0:T(8,128)(2,1)S(1)}, u32[]{:S(2)}, u32[]{:S(2)}) collective-permute-start(bf16[2,2,128,128]{3,2,1,0:T(8,128)(2,1)S(1)} %maximum_bitcast_fusion.refs_0_), channel_id=1, source_target_pairs={{0,12},{2,14},{4,8},{6,10},{8,4},{10,6},{12,0},{14,2},{16,28},{18,... | collective-permute-start | bytes 393224 | tf_op jit(solution)/shard_map/ppermute | solution.py:257
  1.0 10.2 %collective-permute-start.1 = (bf16[2,2,128,128]{3,2,1,0:T(8,128)(2,1)S(1)}, bf16[2,2,128,128]{3,2,1,0:T(8,128)(2,1)S(1)}, u32[]{:S(2)}, u32[]{:S(2)}) collective-permute-start(bf16[2,2,128,128]{3,2,1,0:T(8,128)(2,1)S(1)} %maximum_bitcast_fusion.refs_0_), channel_id=1, source_target_pairs={{0,6},{2,4},{4,2},{6,0},{8,14},{10,12},{12,10},{14,8},{16,22},{18,... | collective-permute-start | bytes 393224 | tf_op jit(solution)/shard_map/ppermute | solution.py:257
  2.8 11.0 %collective-permute-start.2 = (bf16[2,2,128,128]{3,2,1,0:T(8,128)(2,1)S(1)}, bf16[2,2,128,128]{3,2,1,0:T(8,128)(2,1)S(1)}, u32[]{:S(2)}, u32[]{:S(2)}) collective-permute-start(bf16[2,2,128,128]{3,2,1,0:T(8,128)(2,1)S(1)} %maximum_bitcast_fusion.refs_0_), channel_id=1, source_target_pairs={{0,4},{2,6},{4,0},{6,2},{8,12},{10,14},{12,8},{14,10},{16,20},{18,... | collective-permute-start | bytes 393224 | tf_op jit(solution)/shard_map/ppermute | solution.py:257
  4.2 9.6 %collective-permute-start.3 = (bf16[2,2,128,128]{3,2,1,0:T(8,128)(2,1)S(1)}, bf16[2,2,128,128]{3,2,1,0:T(8,128)(2,1)S(1)}, u32[]{:S(2)}, u32[]{:S(2)}) collective-permute-start(bf16[2,2,128,128]{3,2,1,0:T(8,128)(2,1)S(1)} %maximum_bitcast_fusion.refs_0_), channel_id=1, source_target_pairs={{0,2},{2,0},{4,6},{6,4},{8,10},{10,8},{12,14},{14,12},{16,18},{18,... | collective-permute-start | bytes 393224 | tf_op jit(solution)/shard_map/ppermute | solution.py:257
  9.2 6.9 %collective-permute-start.4 = (bf16[2,2,128,128]{3,2,1,0:T(8,128)(2,1)S(1)}, bf16[2,2,128,128]{3,2,1,0:T(8,128)(2,1)S(1)}, u32[]{:S(2)}, u32[]{:S(2)}) collective-permute-start(bf16[2,2,128,128]{3,2,1,0:T(8,128)(2,1)S(1)} %collective-permute-done.refs_4_), channel_id=1, source_target_pairs={{0,2},{2,0},{4,6},{6,4},{8,10},{10,8},{12,14},{14,12},{16,18},{18,... | collective-permute-start | bytes 393224 | tf_op jit(solution)/shard_map/ppermute | solution.py:257
  10.7 6.4 %collective-permute-start.5 = (bf16[2,2,128,128]{3,2,1,0:T(8,128)(2,1)S(1)}, bf16[2,2,128,128]{3,2,1,0:T(8,128)(2,1)S(1)}, u32[]{:S(2)}, u32[]{:S(2)}) collective-permute-start(bf16[2,2,128,128]{3,2,1,0:T(8,128)(2,1)S(1)} %collective-permute-done.refs_4_), channel_id=1, source_target_pairs={{0,16},{2,18},{4,20},{6,22},{8,14},{10,12},{12,10},{14,8},{16,0},{... | collective-permute-start | bytes 393224 | tf_op jit(solution)/shard_map/ppermute | solution.py:257
  11.2 7.3 %collective-permute-start.6 = (bf16[2,2,128,128]{3,2,1,0:T(8,128)(2,1)S(1)}, bf16[2,2,128,128]{3,2,1,0:T(8,128)(2,1)S(1)}, u32[]{:S(2)}, u32[]{:S(2)}) collective-permute-start(bf16[2,2,128,128]{3,2,1,0:T(8,128)(2,1)S(1)} %collective-permute-done.refs_4_), channel_id=1, source_target_pairs={{0,4},{2,6},{4,0},{6,2},{8,12},{10,14},{12,8},{14,10},{16,20},{18,... | collective-permute-start | bytes 393224 | tf_op jit(solution)/shard_map/ppermute | solution.py:257
